TPU v7x, 256 devices: a whole 4x4x8 slice. The times are simulated.
256 devices in a mesh: slab: 16 (over y, x), energy: 8 (over z), mom: 2 (over core).
Axes of the slice: x: 4, y: 4, z: 8, core: 2. Of those that a mesh axis runs over, the one named last changes fastest.
Arguments:
- onsite: float32 [2, 16, 256], P('mom', 'slab'), may hold values from -0.5 to 0.5
- hop: float32 [2, 16, 2, 256, 256], P('mom', 'slab'), may hold values from -0.0234375 to 0.0234375
- couple: float32 [2, 16, 2, 256, 256], P('mom', 'slab'), may hold values from -2 to 2
- sigma_in: float32 [16, 16, 2, 256, 256], P('energy', 'slab'), may hold values from -0.03125 to 0.03125
- shifts: int32 [4], replicated, may hold values from 1 to 15
- mode_weight: float32 [2, 4], replicated, may hold values from 0.2 to 1
Outputs:
- sigma_out: float32 [16, 16, 2, 256, 256], P(None, 'slab', None, 'energy')
Inputs may be any that keep to these rules, and one draw needn't show every extreme that they name: `shifts`: energy-index offsets of the phonon modes.
All inputs are finite; a program needn't handle non-finite values.
Results may differ from a plain program's by a relative error of at most 0.00025.
Values sent between devices are 32-bit elements; how exact they have to be, the bound alone decides.
A program may use at most 128 MiB of HBM per device.

v0:
```python
import jax
import jax.numpy as jnp
from jax import lax
from jax.sharding import PartitionSpec as P

ETA = 0.5
HIGH = lax.Precision.HIGHEST


def shifted(shard, axis, by):
    length = lax.axis_size(axis)
    pairs = [(i, i + by) for i in range(length) if 0 <= i + by < length]
    return lax.ppermute(shard, axis, pairs)


def complex_mul(form, left, right):

    def product(first, second):
        return jnp.einsum(form, first, second, precision=HIGH)

    return (
        product(left[0], right[0]) - product(left[1], right[1]),
        product(left[0], right[1]) + product(left[1], right[0]),
    )


def newton_inverse(mat_real, mat_imag, form, identity):
    diag_real = jnp.diagonal(mat_real, axis1=-2, axis2=-1)
    diag_imag = jnp.diagonal(mat_imag, axis1=-2, axis2=-1)
    denom = diag_real * diag_real + diag_imag * diag_imag
    x_real = diag_real / denom
    x_imag = -diag_imag / denom
    rows_real = x_real[..., :, None] * mat_real - x_imag[..., :, None] * mat_imag
    rows_imag = x_real[..., :, None] * mat_imag + x_imag[..., :, None] * mat_real
    both_real = rows_real * x_real[..., None, :] - rows_imag * x_imag[..., None, :]
    both_imag = rows_real * x_imag[..., None, :] + rows_imag * x_real[..., None, :]
    first = (
        2.0 * identity * x_real[..., None, :] - both_real,
        2.0 * identity * x_imag[..., None, :] - both_imag,
    )
    resid = complex_mul(form, (mat_real, mat_imag), first)
    second = complex_mul(form, first, resid)
    return (2.0 * first[0] - second[0], 2.0 * first[1] - second[1])


def phonon_matrix(shifts, mode_weight, count):
    rows = jnp.arange(count)[:, None, None]
    cols = jnp.arange(count)[None, :, None]
    offset = shifts[None, None, :]
    upper = (cols == rows + offset).astype(jnp.float32)
    lower = (cols == rows - offset).astype(jnp.float32)
    return jnp.sum(upper * mode_weight[0] + lower * mode_weight[1], axis=2)


def body(onsite, hop, couple, sigma_in, shifts, mode_weight):
    e_local = sigma_in.shape[0]
    width = onsite.shape[-1]
    slab_count = lax.axis_size("slab")
    slab_index = lax.axis_index("slab")
    energy_count = lax.axis_size("energy")
    mom_count = lax.axis_size("mom")
    total = e_local * energy_count
    identity = jnp.eye(width, dtype=jnp.float32)
    global_index = lax.axis_index("energy") * e_local + jnp.arange(e_local)
    energy = -0.5 + (global_index.astype(jnp.float32) + 0.5) / total
    coupling = (couple[0, 0, 0], couple[0, 0, 1])
    adjoint = (coupling[0].T, -coupling[1].T)
    hopping = (hop[0, 0, 0], hop[0, 0, 1])
    level = onsite[0, 0]
    sigma = sigma_in[:, 0]

    def forward(received, energies, sig):
        temp = complex_mul("ij,ejl->eil", coupling, (received[:, 0], received[:, 1]))
        left = complex_mul("eij,jl->eil", temp, adjoint)
        z_real = energies[:, None] - level[None, :]
        mat_real = identity * z_real[:, None, :] - hopping[0] - sig[:, 0] - left[0]
        mat_imag = identity * ETA - hopping[1] - sig[:, 1] - left[1]
        green = newton_inverse(mat_real, mat_imag, "eij,ejl->eil", identity)
        return jnp.stack(green, axis=1)

    def backward(green, received):
        pair = (green[:, 0], green[:, 1])
        temp = complex_mul("eij,ejl->eil", pair, (received[:, 0], received[:, 1]))
        extra = complex_mul("eij,ejl->eil", temp, pair)
        full = (pair[0] + extra[0], pair[1] + extra[1])
        temp = complex_mul("ij,ejl->eil", adjoint, full)
        coupled = complex_mul("eij,jl->eil", temp, coupling)
        return (jnp.stack(full, axis=1), jnp.stack(coupled, axis=1))

    empty = jnp.zeros((e_local, 2, width, width), jnp.float32)

    def forward_step(step, green_all):
        received = shifted(green_all, "slab", 1)
        return lax.cond(
            slab_index == step, lambda: forward(received, energy, sigma), lambda: green_all
        )

    green_all = lax.fori_loop(0, slab_count, forward_step, empty)

    def backward_step(step, carry):
        received = shifted(carry[1], "slab", -1)
        return lax.cond(
            slab_index == slab_count - 1 - step,
            lambda: backward(green_all, received),
            lambda: carry,
        )

    full_all, coupled_all = lax.fori_loop(0, slab_count, backward_step, (empty, empty))
    phonon = phonon_matrix(shifts, mode_weight, total)
    blocks = full_all[:, None]
    mixed = jnp.einsum(
        "ef,fsrjl->esrjl",
        phonon,
        lax.all_to_all(blocks, "energy", split_axis=3, concat_axis=0, tiled=True),
        precision=HIGH,
    )
    result = lax.psum(mixed, "mom") / mom_count
    return result


def solution(mesh):
    in_specs = (
        P("mom", "slab", None),
        P("mom", "slab", None, None, None),
        P("mom", "slab", None, None, None),
        P("energy", "slab", None, None, None),
        P(),
        P(),
    )
    out_specs = P(None, "slab", None, "energy", None)
    return jax.shard_map(body, mesh=mesh, in_specs=in_specs, out_specs=out_specs, check_vma=False)
```

profile of v0, /device:TPU:1, one launch (start us, length us, event | category | flops | bytes accessed | tf_op | source)
XLA Modules:
  0.0 1810.3 jit_solution(6463652476634387747)
XLA Ops:
  12.0 770.7 %while.34 = (s32[]{:T(128)}, f32[2,2,256,256]{3,2,0,1:T(8,128)S(1)}, s32[]{:T(128)}, f32[1,1,256]{2,1,0:T(1,128)}, f32[1,1,1,256,256]{4,3,2,1,0:T(8,128)}, /*ind...) while((s32[]{:T(128)}, ...), condition=%wide.region_4.5_spmd.clone.clone, body=%wide.region_1.4_spmd.clone.clone.sunk | while | flops 6447567360 | bytes 44865880 | solution.py:98
  17.4 22.0 %collective-permute-done.1 = f32[2,2,256,256]{2,3,0,1:T(8,128)S(1)} collective-permute-done((f32[2,2,256,256]{2,3,0,1:T(8,128)}, f32[2,2,256,256]{2,3,0,1:T(8,128)S(1)}, u32[]{:S(2)}, u32[]{:S(2)}) %collective-permute-start.1) | collective-permute-done | bytes 1048608 | tf_op jit(solution)/shard_map/while/body/eval_jaxpr/ppermute | solution.py:13
  39.4 53.2 %conditional.7 = (f32[2,2,256,256]{3,2,0,1:T(8,128)S(1)}) conditional(s32[]{:T(128)} %convert_element_type.49, f32[2,2,256,256]{3,2,0,1:T(8,128)S(1)} %get-tuple-element.764, (f32[256,256]{1,0:T(8,128)S(1)}, f32[256,256]{1,0:T(8,128)S(1)}, f32[256,256]{1,0:T(8,128)S(1)}, f32[2]{0:T(128)S(1)}, f32[1,1,256]{2,1,0:T(1,128)}, ...), branch_computations={%region_2.2_spmd, %region_3.3_spmd.clone} | conditional | flops 6447436288 | bytes 38311968 | solution.py:94
  49.0 16.5 copy.145
  67.9 16.5 copy.143
  95.3 21.4 %collective-permute-done.1 = f32[2,2,256,256]{2,3,0,1:T(8,128)S(1)} collective-permute-done((f32[2,2,256,256]{2,3,0,1:T(8,128)}, f32[2,2,256,256]{2,3,0,1:T(8,128)S(1)}, u32[]{:S(2)}, u32[]{:S(2)}) %collective-permute-start.1) | collective-permute-done | bytes 1048608 | tf_op jit(solution)/shard_map/while/body/eval_jaxpr/ppermute | solution.py:13
  118.0 57.2 %collective-permute-start.1 = (f32[2,2,256,256]{2,3,0,1:T(8,128)}, f32[2,2,256,256]{2,3,0,1:T(8,128)S(1)}, u32[]{:S(2)}, u32[]{:S(2)}) collective-permute-start(f32[2,2,256,256]{2,3,0,1:T(8,128)} %copy.154), channel_id=1, source_target_pairs={{0,16},{16,32},{32,48},{48,64},{64,80},{80,96},{96,112},{112,128},... | collective-permute-start | bytes 3145736 | tf_op jit(solution)/shard_map/while/body/eval_jaxpr/ppermute | solution.py:13
  175.3 20.4 %collective-permute-done.1 = f32[2,2,256,256]{2,3,0,1:T(8,128)S(1)} collective-permute-done((f32[2,2,256,256]{2,3,0,1:T(8,128)}, f32[2,2,256,256]{2,3,0,1:T(8,128)S(1)}, u32[]{:S(2)}, u32[]{:S(2)}) %collective-permute-start.1) | collective-permute-done | bytes 1048608 | tf_op jit(solution)/shard_map/while/body/eval_jaxpr/ppermute | solution.py:13
  201.2 19.5 %collective-permute-done.1 = f32[2,2,256,256]{2,3,0,1:T(8,128)S(1)} collective-permute-done((f32[2,2,256,256]{2,3,0,1:T(8,128)}, f32[2,2,256,256]{2,3,0,1:T(8,128)S(1)}, u32[]{:S(2)}, u32[]{:S(2)}) %collective-permute-start.1) | collective-permute-done | bytes 1048608 | tf_op jit(solution)/shard_map/while/body/eval_jaxpr/ppermute | solution.py:13
  222.0 55.7 %collective-permute-start.1 = (f32[2,2,256,256]{2,3,0,1:T(8,128)}, f32[2,2,256,256]{2,3,0,1:T(8,128)S(1)}, u32[]{:S(2)}, u32[]{:S(2)}) collective-permute-start(f32[2,2,256,256]{2,3,0,1:T(8,128)} %copy.154), channel_id=1, source_target_pairs={{0,16},{16,32},{32,48},{48,64},{64,80},{80,96},{96,112},{112,128},... | collective-permute-start | bytes 3145736 | tf_op jit(solution)/shard_map/while/body/eval_jaxpr/ppermute | solution.py:13
  277.8 18.9 %collective-permute-done.1 = f32[2,2,256,256]{2,3,0,1:T(8,128)S(1)} collective-permute-done((f32[2,2,256,256]{2,3,0,1:T(8,128)}, f32[2,2,256,256]{2,3,0,1:T(8,128)S(1)}, u32[]{:S(2)}, u32[]{:S(2)}) %collective-permute-start.1) | collective-permute-done | bytes 1048608 | tf_op jit(solution)/shard_map/while/body/eval_jaxpr/ppermute | solution.py:13
  302.1 17.9 collective-permute-done.1
  321.4 56.0 %collective-permute-start.1 = (f32[2,2,256,256]{2,3,0,1:T(8,128)}, f32[2,2,256,256]{2,3,0,1:T(8,128)S(1)}, u32[]{:S(2)}, u32[]{:S(2)}) collective-permute-start(f32[2,2,256,256]{2,3,0,1:T(8,128)} %copy.154), channel_id=1, source_target_pairs={{0,16},{16,32},{32,48},{48,64},{64,80},{80,96},{96,112},{112,128},... | collective-permute-start | bytes 3145736 | tf_op jit(solution)/shard_map/while/body/eval_jaxpr/ppermute | solution.py:13
  377.5 17.3 collective-permute-done.1
  400.2 16.4 collective-permute-done.1
  417.9 58.4 %collective-permute-start.1 = (f32[2,2,256,256]{2,3,0,1:T(8,128)}, f32[2,2,256,256]{2,3,0,1:T(8,128)S(1)}, u32[]{:S(2)}, u32[]{:S(2)}) collective-permute-start(f32[2,2,256,256]{2,3,0,1:T(8,128)} %copy.154), channel_id=1, source_target_pairs={{0,16},{16,32},{32,48},{48,64},{64,80},{80,96},{96,112},{112,128},... | collective-permute-start | bytes 3145736 | tf_op jit(solution)/shard_map/while/body/eval_jaxpr/ppermute | solution.py:13
  476.4 15.8 collective-permute-done.1
  499.7 14.8 collective-permute-done.1
  515.9 54.4 %collective-permute-start.1 = (f32[2,2,256,256]{2,3,0,1:T(8,128)}, f32[2,2,256,256]{2,3,0,1:T(8,128)S(1)}, u32[]{:S(2)}, u32[]{:S(2)}) collective-permute-start(f32[2,2,256,256]{2,3,0,1:T(8,128)} %copy.154), channel_id=1, source_target_pairs={{0,16},{16,32},{32,48},{48,64},{64,80},{80,96},{96,112},{112,128},... | collective-permute-start | bytes 3145736 | tf_op jit(solution)/shard_map/while/body/eval_jaxpr/ppermute | solution.py:13
  570.4 14.2 collective-permute-done.1
  592.1 14.8 collective-permute-done.1
  608.2 50.2 %collective-permute-start.1 = (f32[2,2,256,256]{2,3,0,1:T(8,128)}, f32[2,2,256,256]{2,3,0,1:T(8,128)S(1)}, u32[]{:S(2)}, u32[]{:S(2)}) collective-permute-start(f32[2,2,256,256]{2,3,0,1:T(8,128)} %copy.154), channel_id=1, source_target_pairs={{0,16},{16,32},{32,48},{48,64},{64,80},{80,96},{96,112},{112,128},... | collective-permute-start | bytes 3145736 | tf_op jit(solution)/shard_map/while/body/eval_jaxpr/ppermute | solution.py:13
  658.4 11.9 collective-permute-done.1
  682.0 11.9 collective-permute-done.1
  695.2 50.6 %collective-permute-start.1 = (f32[2,2,256,256]{2,3,0,1:T(8,128)}, f32[2,2,256,256]{2,3,0,1:T(8,128)S(1)}, u32[]{:S(2)}, u32[]{:S(2)}) collective-permute-start(f32[2,2,256,256]{2,3,0,1:T(8,128)} %copy.154), channel_id=1, source_target_pairs={{0,16},{16,32},{32,48},{48,64},{64,80},{80,96},{96,112},{112,128},... | collective-permute-start | bytes 3145736 | tf_op jit(solution)/shard_map/while/body/eval_jaxpr/ppermute | solution.py:13
  745.9 11.9 collective-permute-done.1
  759.1 11.6 collective-permute-start.1
  770.8 11.9 collective-permute-done.1
  784.8 916.4 %while.33 = (s32[]{:T(128)}, f32[2,2,256,256]{3,2,0,1:T(8,128)}, f32[2,2,256,256]{3,2,0,1:T(8,128)}, s32[]{:T(128)}, f32[2,2,256,256]{3,2,0,1:T(8,128)S(1)}, /*i...) while((s32[]{:T(128)}, f32[2,2,256,256]{3,2,0,1:T(8,128)}, ...), condition=%wide.region_8.9_spmd, body=%wide.region_5.8_spmd.sunk | while | flops 6444285952 | bytes 36700408 | solution.py:108
  786.3 65.2 %collective-permute-done = f32[2,2,256,256]{3,2,0,1:T(8,128)S(1)} collective-permute-done((f32[2,2,256,256]{3,2,0,1:T(8,128)}, f32[2,2,256,256]{3,2,0,1:T(8,128)S(1)}, u32[]{:S(2)}, u32[]{:S(2)}) %collective-permute-start) | collective-permute-done | bytes 1048608 | tf_op jit(solution)/shard_map/while/body/eval_jaxpr/ppermute | solution.py:13
  852.7 24.9 %collective-permute-done = f32[2,2,256,256]{3,2,0,1:T(8,128)S(1)} collective-permute-done((f32[2,2,256,256]{3,2,0,1:T(8,128)}, f32[2,2,256,256]{3,2,0,1:T(8,128)S(1)}, u32[]{:S(2)}, u32[]{:S(2)}) %collective-permute-start) | collective-permute-done | bytes 1048608 | tf_op jit(solution)/shard_map/while/body/eval_jaxpr/ppermute | solution.py:13
  878.9 55.1 %collective-permute-done = f32[2,2,256,256]{3,2,0,1:T(8,128)S(1)} collective-permute-done((f32[2,2,256,256]{3,2,0,1:T(8,128)}, f32[2,2,256,256]{3,2,0,1:T(8,128)S(1)}, u32[]{:S(2)}, u32[]{:S(2)}) %collective-permute-start) | collective-permute-done | bytes 1048608 | tf_op jit(solution)/shard_map/while/body/eval_jaxpr/ppermute | solution.py:13
  935.3 36.3 %collective-permute-done = f32[2,2,256,256]{3,2,0,1:T(8,128)S(1)} collective-permute-done((f32[2,2,256,256]{3,2,0,1:T(8,128)}, f32[2,2,256,256]{3,2,0,1:T(8,128)S(1)}, u32[]{:S(2)}, u32[]{:S(2)}) %collective-permute-start) | collective-permute-done | bytes 1048608 | tf_op jit(solution)/shard_map/while/body/eval_jaxpr/ppermute | solution.py:13
  972.9 47.2 %collective-permute-done = f32[2,2,256,256]{3,2,0,1:T(8,128)S(1)} collective-permute-done((f32[2,2,256,256]{3,2,0,1:T(8,128)}, f32[2,2,256,256]{3,2,0,1:T(8,128)S(1)}, u32[]{:S(2)}, u32[]{:S(2)}) %collective-permute-start) | collective-permute-done | bytes 1048608 | tf_op jit(solution)/shard_map/while/body/eval_jaxpr/ppermute | solution.py:13
  1021.4 33.9 %collective-permute-done = f32[2,2,256,256]{3,2,0,1:T(8,128)S(1)} collective-permute-done((f32[2,2,256,256]{3,2,0,1:T(8,128)}, f32[2,2,256,256]{3,2,0,1:T(8,128)S(1)}, u32[]{:S(2)}, u32[]{:S(2)}) %collective-permute-start) | collective-permute-done | bytes 1048608 | tf_op jit(solution)/shard_map/while/body/eval_jaxpr/ppermute | solution.py:13
  1056.6 49.7 %collective-permute-done = f32[2,2,256,256]{3,2,0,1:T(8,128)S(1)} collective-permute-done((f32[2,2,256,256]{3,2,0,1:T(8,128)}, f32[2,2,256,256]{3,2,0,1:T(8,128)S(1)}, u32[]{:S(2)}, u32[]{:S(2)}) %collective-permute-start) | collective-permute-done | bytes 1048608 | tf_op jit(solution)/shard_map/while/body/eval_jaxpr/ppermute | solution.py:13
  1107.6 38.9 %collective-permute-done = f32[2,2,256,256]{3,2,0,1:T(8,128)S(1)} collective-permute-done((f32[2,2,256,256]{3,2,0,1:T(8,128)}, f32[2,2,256,256]{3,2,0,1:T(8,128)S(1)}, u32[]{:S(2)}, u32[]{:S(2)}) %collective-permute-start) | collective-permute-done | bytes 1048608 | tf_op jit(solution)/shard_map/while/body/eval_jaxpr/ppermute | solution.py:13
  1147.8 46.2 %collective-permute-done = f32[2,2,256,256]{3,2,0,1:T(8,128)S(1)} collective-permute-done((f32[2,2,256,256]{3,2,0,1:T(8,128)}, f32[2,2,256,256]{3,2,0,1:T(8,128)S(1)}, u32[]{:S(2)}, u32[]{:S(2)}) %collective-permute-start) | collective-permute-done | bytes 1048608 | tf_op jit(solution)/shard_map/while/body/eval_jaxpr/ppermute | solution.py:13
  1195.3 39.7 %collective-permute-done = f32[2,2,256,256]{3,2,0,1:T(8,128)S(1)} collective-permute-done((f32[2,2,256,256]{3,2,0,1:T(8,128)}, f32[2,2,256,256]{3,2,0,1:T(8,128)S(1)}, u32[]{:S(2)}, u32[]{:S(2)}) %collective-permute-start) | collective-permute-done | bytes 1048608 | tf_op jit(solution)/shard_map/while/body/eval_jaxpr/ppermute | solution.py:13
  1236.3 42.7 %collective-permute-done = f32[2,2,256,256]{3,2,0,1:T(8,128)S(1)} collective-permute-done((f32[2,2,256,256]{3,2,0,1:T(8,128)}, f32[2,2,256,256]{3,2,0,1:T(8,128)S(1)}, u32[]{:S(2)}, u32[]{:S(2)}) %collective-permute-start) | collective-permute-done | bytes 1048608 | tf_op jit(solution)/shard_map/while/body/eval_jaxpr/ppermute | solution.py:13
  1280.3 121.5 %collective-permute-done = f32[2,2,256,256]{3,2,0,1:T(8,128)S(1)} collective-permute-done((f32[2,2,256,256]{3,2,0,1:T(8,128)}, f32[2,2,256,256]{3,2,0,1:T(8,128)S(1)}, u32[]{:S(2)}, u32[]{:S(2)}) %collective-permute-start) | collective-permute-done | bytes 1048608 | tf_op jit(solution)/shard_map/while/body/eval_jaxpr/ppermute | solution.py:13
  1403.2 23.5 %collective-permute-done = f32[2,2,256,256]{3,2,0,1:T(8,128)S(1)} collective-permute-done((f32[2,2,256,256]{3,2,0,1:T(8,128)}, f32[2,2,256,256]{3,2,0,1:T(8,128)S(1)}, u32[]{:S(2)}, u32[]{:S(2)}) %collective-permute-start) | collective-permute-done | bytes 1048608 | tf_op jit(solution)/shard_map/while/body/eval_jaxpr/ppermute | solution.py:13
  1428.0 69.4 %collective-permute-done = f32[2,2,256,256]{3,2,0,1:T(8,128)S(1)} collective-permute-done((f32[2,2,256,256]{3,2,0,1:T(8,128)}, f32[2,2,256,256]{3,2,0,1:T(8,128)S(1)}, u32[]{:S(2)}, u32[]{:S(2)}) %collective-permute-start) | collective-permute-done | bytes 1048608 | tf_op jit(solution)/shard_map/while/body/eval_jaxpr/ppermute | solution.py:13
  1498.6 22.4 %collective-permute-done = f32[2,2,256,256]{3,2,0,1:T(8,128)S(1)} collective-permute-done((f32[2,2,256,256]{3,2,0,1:T(8,128)}, f32[2,2,256,256]{3,2,0,1:T(8,128)S(1)}, u32[]{:S(2)}, u32[]{:S(2)}) %collective-permute-start) | collective-permute-done | bytes 1048608 | tf_op jit(solution)/shard_map/while/body/eval_jaxpr/ppermute | solution.py:13
  1522.3 163.8 %collective-permute-done = f32[2,2,256,256]{3,2,0,1:T(8,128)S(1)} collective-permute-done((f32[2,2,256,256]{3,2,0,1:T(8,128)}, f32[2,2,256,256]{3,2,0,1:T(8,128)S(1)}, u32[]{:S(2)}, u32[]{:S(2)}) %collective-permute-start) | collective-permute-done | bytes 1048608 | tf_op jit(solution)/shard_map/while/body/eval_jaxpr/ppermute | solution.py:13
  1686.2 15.1 conditional.6
  1713.0 17.6 all-to-all-done
  1733.9 66.7 %all-reduce.2.cloned.1.call-done = f32[16,1,2,32,256]{4,0,3,2,1:T(8,128)} async-done(((f32[16,1,2,32,256]{4,0,3,2,1:T(8,128)}), f32[16,1,2,32,256]{4,0,3,2,1:T(8,128)}) %all-reduce.2.cloned.1.call-update) | async-done | bytes 1048592 | tf_op jit(solution)/shard_map/psum | solution.py:117
  (172 shorter events, 142.8 us)
Async XLA Ops:
  13.4 26.1 %collective-permute-start.1 = (f32[2,2,256,256]{2,3,0,1:T(8,128)}, f32[2,2,256,256]{2,3,0,1:T(8,128)S(1)}, u32[]{:S(2)}, u32[]{:S(2)}) collective-permute-start(f32[2,2,256,256]{2,3,0,1:T(8,128)} %copy.154), channel_id=1, source_target_pairs={{0,16},{16,32},{32,48},{48,64},{64,80},{80,96},{96,112},{112,128},... | collective-permute-start | bytes 3145736 | tf_op jit(solution)/shard_map/while/body/eval_jaxpr/ppermute | solution.py:13
  94.0 22.8 %collective-permute-start.1 = (f32[2,2,256,256]{2,3,0,1:T(8,128)}, f32[2,2,256,256]{2,3,0,1:T(8,128)S(1)}, u32[]{:S(2)}, u32[]{:S(2)}) collective-permute-start(f32[2,2,256,256]{2,3,0,1:T(8,128)} %copy.154), channel_id=1, source_target_pairs={{0,16},{16,32},{32,48},{48,64},{64,80},{80,96},{96,112},{112,128},... | collective-permute-start | bytes 3145736 | tf_op jit(solution)/shard_map/while/body/eval_jaxpr/ppermute | solution.py:13
  118.0 77.7 %collective-permute-start.1 = (f32[2,2,256,256]{2,3,0,1:T(8,128)}, f32[2,2,256,256]{2,3,0,1:T(8,128)S(1)}, u32[]{:S(2)}, u32[]{:S(2)}) collective-permute-start(f32[2,2,256,256]{2,3,0,1:T(8,128)} %copy.154), channel_id=1, source_target_pairs={{0,16},{16,32},{32,48},{48,64},{64,80},{80,96},{96,112},{112,128},... | collective-permute-start | bytes 3145736 | tf_op jit(solution)/shard_map/while/body/eval_jaxpr/ppermute | solution.py:13
  197.1 23.6 %collective-permute-start.1 = (f32[2,2,256,256]{2,3,0,1:T(8,128)}, f32[2,2,256,256]{2,3,0,1:T(8,128)S(1)}, u32[]{:S(2)}, u32[]{:S(2)}) collective-permute-start(f32[2,2,256,256]{2,3,0,1:T(8,128)} %copy.154), channel_id=1, source_target_pairs={{0,16},{16,32},{32,48},{48,64},{64,80},{80,96},{96,112},{112,128},... | collective-permute-start | bytes 3145736 | tf_op jit(solution)/shard_map/while/body/eval_jaxpr/ppermute | solution.py:13
  222.0 74.7 %collective-permute-start.1 = (f32[2,2,256,256]{2,3,0,1:T(8,128)}, f32[2,2,256,256]{2,3,0,1:T(8,128)S(1)}, u32[]{:S(2)}, u32[]{:S(2)}) collective-permute-start(f32[2,2,256,256]{2,3,0,1:T(8,128)} %copy.154), channel_id=1, source_target_pairs={{0,16},{16,32},{32,48},{48,64},{64,80},{80,96},{96,112},{112,128},... | collective-permute-start | bytes 3145736 | tf_op jit(solution)/shard_map/while/body/eval_jaxpr/ppermute | solution.py:13
  298.0 22.1 %collective-permute-start.1 = (f32[2,2,256,256]{2,3,0,1:T(8,128)}, f32[2,2,256,256]{2,3,0,1:T(8,128)S(1)}, u32[]{:S(2)}, u32[]{:S(2)}) collective-permute-start(f32[2,2,256,256]{2,3,0,1:T(8,128)} %copy.154), channel_id=1, source_target_pairs={{0,16},{16,32},{32,48},{48,64},{64,80},{80,96},{96,112},{112,128},... | collective-permute-start | bytes 3145736 | tf_op jit(solution)/shard_map/while/body/eval_jaxpr/ppermute | solution.py:13
  321.4 73.4 %collective-permute-start.1 = (f32[2,2,256,256]{2,3,0,1:T(8,128)}, f32[2,2,256,256]{2,3,0,1:T(8,128)S(1)}, u32[]{:S(2)}, u32[]{:S(2)}) collective-permute-start(f32[2,2,256,256]{2,3,0,1:T(8,128)} %copy.154), channel_id=1, source_target_pairs={{0,16},{16,32},{32,48},{48,64},{64,80},{80,96},{96,112},{112,128},... | collective-permute-start | bytes 3145736 | tf_op jit(solution)/shard_map/while/body/eval_jaxpr/ppermute | solution.py:13
  396.1 20.5 %collective-permute-start.1 = (f32[2,2,256,256]{2,3,0,1:T(8,128)}, f32[2,2,256,256]{2,3,0,1:T(8,128)S(1)}, u32[]{:S(2)}, u32[]{:S(2)}) collective-permute-start(f32[2,2,256,256]{2,3,0,1:T(8,128)} %copy.154), channel_id=1, source_target_pairs={{0,16},{16,32},{32,48},{48,64},{64,80},{80,96},{96,112},{112,128},... | collective-permute-start | bytes 3145736 | tf_op jit(solution)/shard_map/while/body/eval_jaxpr/ppermute | solution.py:13
  417.9 74.2 %collective-permute-start.1 = (f32[2,2,256,256]{2,3,0,1:T(8,128)}, f32[2,2,256,256]{2,3,0,1:T(8,128)S(1)}, u32[]{:S(2)}, u32[]{:S(2)}) collective-permute-start(f32[2,2,256,256]{2,3,0,1:T(8,128)} %copy.154), channel_id=1, source_target_pairs={{0,16},{16,32},{32,48},{48,64},{64,80},{80,96},{96,112},{112,128},... | collective-permute-start | bytes 3145736 | tf_op jit(solution)/shard_map/while/body/eval_jaxpr/ppermute | solution.py:13
  493.5 21.0 %collective-permute-start.1 = (f32[2,2,256,256]{2,3,0,1:T(8,128)}, f32[2,2,256,256]{2,3,0,1:T(8,128)S(1)}, u32[]{:S(2)}, u32[]{:S(2)}) collective-permute-start(f32[2,2,256,256]{2,3,0,1:T(8,128)} %copy.154), channel_id=1, source_target_pairs={{0,16},{16,32},{32,48},{48,64},{64,80},{80,96},{96,112},{112,128},... | collective-permute-start | bytes 3145736 | tf_op jit(solution)/shard_map/while/body/eval_jaxpr/ppermute | solution.py:13
  515.9 68.7 %collective-permute-start.1 = (f32[2,2,256,256]{2,3,0,1:T(8,128)}, f32[2,2,256,256]{2,3,0,1:T(8,128)S(1)}, u32[]{:S(2)}, u32[]{:S(2)}) collective-permute-start(f32[2,2,256,256]{2,3,0,1:T(8,128)} %copy.154), channel_id=1, source_target_pairs={{0,16},{16,32},{32,48},{48,64},{64,80},{80,96},{96,112},{112,128},... | collective-permute-start | bytes 3145736 | tf_op jit(solution)/shard_map/while/body/eval_jaxpr/ppermute | solution.py:13
  585.9 21.0 %collective-permute-start.1 = (f32[2,2,256,256]{2,3,0,1:T(8,128)}, f32[2,2,256,256]{2,3,0,1:T(8,128)S(1)}, u32[]{:S(2)}, u32[]{:S(2)}) collective-permute-start(f32[2,2,256,256]{2,3,0,1:T(8,128)} %copy.154), channel_id=1, source_target_pairs={{0,16},{16,32},{32,48},{48,64},{64,80},{80,96},{96,112},{112,128},... | collective-permute-start | bytes 3145736 | tf_op jit(solution)/shard_map/while/body/eval_jaxpr/ppermute | solution.py:13
  608.2 62.2 %collective-permute-start.1 = (f32[2,2,256,256]{2,3,0,1:T(8,128)}, f32[2,2,256,256]{2,3,0,1:T(8,128)S(1)}, u32[]{:S(2)}, u32[]{:S(2)}) collective-permute-start(f32[2,2,256,256]{2,3,0,1:T(8,128)} %copy.154), channel_id=1, source_target_pairs={{0,16},{16,32},{32,48},{48,64},{64,80},{80,96},{96,112},{112,128},... | collective-permute-start | bytes 3145736 | tf_op jit(solution)/shard_map/while/body/eval_jaxpr/ppermute | solution.py:13
  671.6 22.2 %collective-permute-start.1 = (f32[2,2,256,256]{2,3,0,1:T(8,128)}, f32[2,2,256,256]{2,3,0,1:T(8,128)S(1)}, u32[]{:S(2)}, u32[]{:S(2)}) collective-permute-start(f32[2,2,256,256]{2,3,0,1:T(8,128)} %copy.154), channel_id=1, source_target_pairs={{0,16},{16,32},{32,48},{48,64},{64,80},{80,96},{96,112},{112,128},... | collective-permute-start | bytes 3145736 | tf_op jit(solution)/shard_map/while/body/eval_jaxpr/ppermute | solution.py:13
  695.2 62.6 %collective-permute-start.1 = (f32[2,2,256,256]{2,3,0,1:T(8,128)}, f32[2,2,256,256]{2,3,0,1:T(8,128)S(1)}, u32[]{:S(2)}, u32[]{:S(2)}) collective-permute-start(f32[2,2,256,256]{2,3,0,1:T(8,128)} %copy.154), channel_id=1, source_target_pairs={{0,16},{16,32},{32,48},{48,64},{64,80},{80,96},{96,112},{112,128},... | collective-permute-start | bytes 3145736 | tf_op jit(solution)/shard_map/while/body/eval_jaxpr/ppermute | solution.py:13
  759.1 23.6 %collective-permute-start.1 = (f32[2,2,256,256]{2,3,0,1:T(8,128)}, f32[2,2,256,256]{2,3,0,1:T(8,128)S(1)}, u32[]{:S(2)}, u32[]{:S(2)}) collective-permute-start(f32[2,2,256,256]{2,3,0,1:T(8,128)} %copy.154), channel_id=1, source_target_pairs={{0,16},{16,32},{32,48},{48,64},{64,80},{80,96},{96,112},{112,128},... | collective-permute-start | bytes 3145736 | tf_op jit(solution)/shard_map/while/body/eval_jaxpr/ppermute | solution.py:13
  784.8 928.0 %copy-start = (f32[2,4]{1,0:T(2,128)S(1)}, f32[2,4]{1,0:T(2,128)}, u32[]{:S(2)}) copy-start(f32[2,4]{1,0:T(2,128)} %param.19) | copy-start | bytes 100
  784.8 928.0 %copy-start.1 = (s32[4]{0:T(128)S(1)}, s32[4]{0:T(128)}, u32[]{:S(2)}) copy-start(s32[4]{0:T(128)} %param.18) | copy-start | bytes 52
  784.8 66.6 %collective-permute-start = (f32[2,2,256,256]{3,2,0,1:T(8,128)}, f32[2,2,256,256]{3,2,0,1:T(8,128)S(1)}, u32[]{:S(2)}, u32[]{:S(2)}) collective-permute-start(f32[2,2,256,256]{3,2,0,1:T(8,128)} %get-tuple-element.802), channel_id=1, source_target_pairs={{16,0},{32,16},{48,32},{64,48},{80,64},{96,80},{112,96},{128,112},... | collective-permute-start | bytes 3145736 | tf_op jit(solution)/shard_map/while/body/eval_jaxpr/ppermute | solution.py:13
  851.4 26.2 %collective-permute-start = (f32[2,2,256,256]{3,2,0,1:T(8,128)}, f32[2,2,256,256]{3,2,0,1:T(8,128)S(1)}, u32[]{:S(2)}, u32[]{:S(2)}) collective-permute-start(f32[2,2,256,256]{3,2,0,1:T(8,128)} %get-tuple-element.802), channel_id=1, source_target_pairs={{16,0},{32,16},{48,32},{64,48},{80,64},{96,80},{112,96},{128,112},... | collective-permute-start | bytes 3145736 | tf_op jit(solution)/shard_map/while/body/eval_jaxpr/ppermute | solution.py:13
  877.6 56.4 %collective-permute-start = (f32[2,2,256,256]{3,2,0,1:T(8,128)}, f32[2,2,256,256]{3,2,0,1:T(8,128)S(1)}, u32[]{:S(2)}, u32[]{:S(2)}) collective-permute-start(f32[2,2,256,256]{3,2,0,1:T(8,128)} %get-tuple-element.802), channel_id=1, source_target_pairs={{16,0},{32,16},{48,32},{64,48},{80,64},{96,80},{112,96},{128,112},... | collective-permute-start | bytes 3145736 | tf_op jit(solution)/shard_map/while/body/eval_jaxpr/ppermute | solution.py:13
  934.0 37.6 %collective-permute-start = (f32[2,2,256,256]{3,2,0,1:T(8,128)}, f32[2,2,256,256]{3,2,0,1:T(8,128)S(1)}, u32[]{:S(2)}, u32[]{:S(2)}) collective-permute-start(f32[2,2,256,256]{3,2,0,1:T(8,128)} %get-tuple-element.802), channel_id=1, source_target_pairs={{16,0},{32,16},{48,32},{64,48},{80,64},{96,80},{112,96},{128,112},... | collective-permute-start | bytes 3145736 | tf_op jit(solution)/shard_map/while/body/eval_jaxpr/ppermute | solution.py:13
  971.6 48.5 %collective-permute-start = (f32[2,2,256,256]{3,2,0,1:T(8,128)}, f32[2,2,256,256]{3,2,0,1:T(8,128)S(1)}, u32[]{:S(2)}, u32[]{:S(2)}) collective-permute-start(f32[2,2,256,256]{3,2,0,1:T(8,128)} %get-tuple-element.802), channel_id=1, source_target_pairs={{16,0},{32,16},{48,32},{64,48},{80,64},{96,80},{112,96},{128,112},... | collective-permute-start | bytes 3145736 | tf_op jit(solution)/shard_map/while/body/eval_jaxpr/ppermute | solution.py:13
  1020.1 35.2 %collective-permute-start = (f32[2,2,256,256]{3,2,0,1:T(8,128)}, f32[2,2,256,256]{3,2,0,1:T(8,128)S(1)}, u32[]{:S(2)}, u32[]{:S(2)}) collective-permute-start(f32[2,2,256,256]{3,2,0,1:T(8,128)} %get-tuple-element.802), channel_id=1, source_target_pairs={{16,0},{32,16},{48,32},{64,48},{80,64},{96,80},{112,96},{128,112},... | collective-permute-start | bytes 3145736 | tf_op jit(solution)/shard_map/while/body/eval_jaxpr/ppermute | solution.py:13
  1055.3 51.0 %collective-permute-start = (f32[2,2,256,256]{3,2,0,1:T(8,128)}, f32[2,2,256,256]{3,2,0,1:T(8,128)S(1)}, u32[]{:S(2)}, u32[]{:S(2)}) collective-permute-start(f32[2,2,256,256]{3,2,0,1:T(8,128)} %get-tuple-element.802), channel_id=1, source_target_pairs={{16,0},{32,16},{48,32},{64,48},{80,64},{96,80},{112,96},{128,112},... | collective-permute-start | bytes 3145736 | tf_op jit(solution)/shard_map/while/body/eval_jaxpr/ppermute | solution.py:13
  1106.3 40.2 %collective-permute-start = (f32[2,2,256,256]{3,2,0,1:T(8,128)}, f32[2,2,256,256]{3,2,0,1:T(8,128)S(1)}, u32[]{:S(2)}, u32[]{:S(2)}) collective-permute-start(f32[2,2,256,256]{3,2,0,1:T(8,128)} %get-tuple-element.802), channel_id=1, source_target_pairs={{16,0},{32,16},{48,32},{64,48},{80,64},{96,80},{112,96},{128,112},... | collective-permute-start | bytes 3145736 | tf_op jit(solution)/shard_map/while/body/eval_jaxpr/ppermute | solution.py:13
  1146.5 47.5 %collective-permute-start = (f32[2,2,256,256]{3,2,0,1:T(8,128)}, f32[2,2,256,256]{3,2,0,1:T(8,128)S(1)}, u32[]{:S(2)}, u32[]{:S(2)}) collective-permute-start(f32[2,2,256,256]{3,2,0,1:T(8,128)} %get-tuple-element.802), channel_id=1, source_target_pairs={{16,0},{32,16},{48,32},{64,48},{80,64},{96,80},{112,96},{128,112},... | collective-permute-start | bytes 3145736 | tf_op jit(solution)/shard_map/while/body/eval_jaxpr/ppermute | solution.py:13
  1194.0 41.0 %collective-permute-start = (f32[2,2,256,256]{3,2,0,1:T(8,128)}, f32[2,2,256,256]{3,2,0,1:T(8,128)S(1)}, u32[]{:S(2)}, u32[]{:S(2)}) collective-permute-start(f32[2,2,256,256]{3,2,0,1:T(8,128)} %get-tuple-element.802), channel_id=1, source_target_pairs={{16,0},{32,16},{48,32},{64,48},{80,64},{96,80},{112,96},{128,112},... | collective-permute-start | bytes 3145736 | tf_op jit(solution)/shard_map/while/body/eval_jaxpr/ppermute | solution.py:13
  1235.0 44.0 %collective-permute-start = (f32[2,2,256,256]{3,2,0,1:T(8,128)}, f32[2,2,256,256]{3,2,0,1:T(8,128)S(1)}, u32[]{:S(2)}, u32[]{:S(2)}) collective-permute-start(f32[2,2,256,256]{3,2,0,1:T(8,128)} %get-tuple-element.802), channel_id=1, source_target_pairs={{16,0},{32,16},{48,32},{64,48},{80,64},{96,80},{112,96},{128,112},... | collective-permute-start | bytes 3145736 | tf_op jit(solution)/shard_map/while/body/eval_jaxpr/ppermute | solution.py:13
  1279.0 122.8 %collective-permute-start = (f32[2,2,256,256]{3,2,0,1:T(8,128)}, f32[2,2,256,256]{3,2,0,1:T(8,128)S(1)}, u32[]{:S(2)}, u32[]{:S(2)}) collective-permute-start(f32[2,2,256,256]{3,2,0,1:T(8,128)} %get-tuple-element.802), channel_id=1, source_target_pairs={{16,0},{32,16},{48,32},{64,48},{80,64},{96,80},{112,96},{128,112},... | collective-permute-start | bytes 3145736 | tf_op jit(solution)/shard_map/while/body/eval_jaxpr/ppermute | solution.py:13
  1401.9 24.8 %collective-permute-start = (f32[2,2,256,256]{3,2,0,1:T(8,128)}, f32[2,2,256,256]{3,2,0,1:T(8,128)S(1)}, u32[]{:S(2)}, u32[]{:S(2)}) collective-permute-start(f32[2,2,256,256]{3,2,0,1:T(8,128)} %get-tuple-element.802), channel_id=1, source_target_pairs={{16,0},{32,16},{48,32},{64,48},{80,64},{96,80},{112,96},{128,112},... | collective-permute-start | bytes 3145736 | tf_op jit(solution)/shard_map/while/body/eval_jaxpr/ppermute | solution.py:13
  1426.7 70.7 %collective-permute-start = (f32[2,2,256,256]{3,2,0,1:T(8,128)}, f32[2,2,256,256]{3,2,0,1:T(8,128)S(1)}, u32[]{:S(2)}, u32[]{:S(2)}) collective-permute-start(f32[2,2,256,256]{3,2,0,1:T(8,128)} %get-tuple-element.802), channel_id=1, source_target_pairs={{16,0},{32,16},{48,32},{64,48},{80,64},{96,80},{112,96},{128,112},... | collective-permute-start | bytes 3145736 | tf_op jit(solution)/shard_map/while/body/eval_jaxpr/ppermute | solution.py:13
  1497.3 23.7 %collective-permute-start = (f32[2,2,256,256]{3,2,0,1:T(8,128)}, f32[2,2,256,256]{3,2,0,1:T(8,128)S(1)}, u32[]{:S(2)}, u32[]{:S(2)}) collective-permute-start(f32[2,2,256,256]{3,2,0,1:T(8,128)} %get-tuple-element.802), channel_id=1, source_target_pairs={{16,0},{32,16},{48,32},{64,48},{80,64},{96,80},{112,96},{128,112},... | collective-permute-start | bytes 3145736 | tf_op jit(solution)/shard_map/while/body/eval_jaxpr/ppermute | solution.py:13
  1521.0 165.1 %collective-permute-start = (f32[2,2,256,256]{3,2,0,1:T(8,128)}, f32[2,2,256,256]{3,2,0,1:T(8,128)S(1)}, u32[]{:S(2)}, u32[]{:S(2)}) collective-permute-start(f32[2,2,256,256]{3,2,0,1:T(8,128)} %get-tuple-element.802), channel_id=1, source_target_pairs={{16,0},{32,16},{48,32},{64,48},{80,64},{96,80},{112,96},{128,112},... | collective-permute-start | bytes 3145736 | tf_op jit(solution)/shard_map/while/body/eval_jaxpr/ppermute | solution.py:13
  1704.2 26.4 %all-to-all-start = ((f32[2,1,2,256,256]{4,0,2,1,3:T(2,128)}), f32[2,1,2,256,256]{4,0,2,1,3:T(2,128)S(1)}, u32[]{:S(2)}, u32[]{:S(2)}) async-start(f32[2,1,2,256,256]{4,0,2,1,3:T(2,128)} %bitcast.207), calls=%async_computation | async-start | bytes 2097152 | tf_op jit(solution)/shard_map/all_to_all | solution.py:114
  1712.8 87.8 %all-reduce.2.cloned.1.call-start = ((), (), s32[]{:S(2)}) async-start(), calls=%async_computation.1 | async-start | bytes 2097152 | tf_op jit(solution)/shard_map/psum | solution.py:117
Sparse Core Ops, SparseCore 0:
  1734.0 66.5 all-reduce.1
where the time goes:
time: 1810 us
  waiting for transfers between devices  1230 us (68%)
  starting transfers between devices  464 us (26%)
  local copies, waits for them, and re-layouts  72.4 us (4%)
  matrix products  29.4 us (2%)
    ppermute x32, waiting for transfers between devices, shifted(): return lax.ppermute(shard, axis, pairs)  1140 us
    ppermute x32, starting transfers between devices, shifted(): return lax.ppermute(shard, axis, pairs)  455 us
    psum x1, waiting for transfers between devices, body(): result = lax.psum(mixed, 'mom') / mom_count  66.7 us
  transfers between devices with their start and end apart: 34, of which 34 were waited for; matrix products, arithmetic and copies ran while one was open for 0% of the time, Pallas kernels for 0%

commit v1 on v0

v1 whole, which is shorter than its diff:
```python
import jax
import jax.numpy as jnp
from jax import lax
from jax.experimental import pallas as pl
from jax.experimental.pallas import tpu as pltpu
from jax.sharding import PartitionSpec as P

ETA = 0.5
HIGH = lax.Precision.HIGHEST
ROW = 4


def split(mat):
    top = mat.astype(jnp.bfloat16)
    return top, (mat - top.astype(jnp.float32)).astype(jnp.bfloat16)


def dot(left, right):
    return jnp.dot(left, right, preferred_element_type=jnp.float32)


def complex_mul(left, right):
    width = left[0].shape[0]
    left_top, left_low = split(jnp.concatenate(left, axis=0))
    outs = []
    for part in right:
        top, low = split(part)
        outs.append(dot(left_top, top) + (dot(left_top, low) + dot(left_low, top)))
    real, imag = outs
    return real[:width] - imag[width:], imag[:width] + real[width:]


def newton_inverse(mat, eye):
    diag_row = tuple(jnp.sum(jnp.where(eye, part, 0.0), axis=0, keepdims=True) for part in mat)
    diag_col = tuple(jnp.sum(jnp.where(eye, part, 0.0), axis=1, keepdims=True) for part in mat)

    def inverse(diag):
        denom = diag[0] * diag[0] + diag[1] * diag[1]
        return diag[0] / denom, -diag[1] / denom

    row, col = inverse(diag_row), inverse(diag_col)
    off = tuple(jnp.where(eye, 0.0, part) for part in mat)
    first = (off[0] * row[0] - off[1] * row[1], off[0] * row[1] + off[1] * row[0])
    second = complex_mul(first, first)
    third = complex_mul(first, second)
    series = (
        jnp.where(eye, 1.0, 0.0) - first[0] + second[0] - third[0],
        second[1] - first[1] - third[1],
    )
    return (
        col[0] * series[0] - col[1] * series[1],
        col[0] * series[1] + col[1] * series[0],
    )


def eye_mask(width):
    shape = (width, width)
    return lax.broadcasted_iota(jnp.int32, shape, 0) == lax.broadcasted_iota(jnp.int32, shape, 1)


def forward_kernel(place, received, bundle, green):
    eye = eye_mask(received.shape[-1])

    def step(j, carry):
        slot = lax.rem(place[0] - j + ROW, ROW)
        coupling = (bundle[slot, 2], bundle[slot, 3])
        adjoint = (bundle[slot, 2].T, -bundle[slot, 3].T)
        left = complex_mul(complex_mul(coupling, carry), adjoint)
        mat = (bundle[slot, 0] - left[0], bundle[slot, 1] - left[1])
        result = newton_inverse(mat, eye)
        green[j, 0] = result[0]
        green[j, 1] = result[1]
        return result

    lax.fori_loop(0, ROW, step, (received[0], received[1]))


def backward_kernel(place, received, bundle, green, full, coupled):

    def step(back, carry):
        j = ROW - 1 - back
        slot = lax.rem(place[0] - j + ROW, ROW)
        pair = (green[j, 0], green[j, 1])
        extra = complex_mul(complex_mul(pair, carry), pair)
        total = (pair[0] + extra[0], pair[1] + extra[1])
        full[j, 0] = total[0]
        full[j, 1] = total[1]
        adjoint = (bundle[slot, 2].T, -bundle[slot, 3].T)
        return complex_mul(complex_mul(adjoint, total), (bundle[slot, 2], bundle[slot, 3]))

    result = lax.fori_loop(0, ROW, step, (received[0], received[1]))
    coupled[0] = result[0]
    coupled[1] = result[1]


def call(kernel, shapes, args):
    specs = [pl.BlockSpec(memory_space=pltpu.SMEM)]
    specs += [pl.BlockSpec(memory_space=pltpu.VMEM)] * (len(args) - 1)
    return pl.pallas_call(
        kernel,
        out_shape=[jax.ShapeDtypeStruct(shape, jnp.float32) for shape in shapes],
        in_specs=specs,
        out_specs=[pl.BlockSpec(memory_space=pltpu.VMEM)] * len(shapes),
        compiler_params=pltpu.CompilerParams(vmem_limit_bytes=48 << 20),
    )(*args)


def phonon_matrix(shifts, mode_weight, count):
    rows = jnp.arange(count)[:, None, None]
    cols = jnp.arange(count)[None, :, None]
    offset = shifts[None, None, :]
    upper = (cols == rows + offset).astype(jnp.float32)
    lower = (cols == rows - offset).astype(jnp.float32)
    return jnp.sum(upper * mode_weight[0] + lower * mode_weight[1], axis=2)


def body(onsite, hop, couple, sigma_in, shifts, mode_weight):
    e_local = sigma_in.shape[0]
    width = onsite.shape[-1]
    slab_count = lax.axis_size("slab")
    rows = slab_count // ROW
    slab = lax.axis_index("slab")
    row, place = slab // ROW, lax.rem(slab, ROW)
    mom = lax.axis_index("mom")
    energy_count = lax.axis_size("energy")
    mom_count = lax.axis_size("mom")
    total = e_local * energy_count
    identity = jnp.eye(width, dtype=jnp.float32)
    global_index = lax.axis_index("energy") * e_local + jnp.arange(e_local)
    energies = -0.5 + (global_index.astype(jnp.float32) + 0.5) / total
    z_real = energies[:, None] - onsite[0, 0][None, :]
    base_real = identity * z_real[:, None, :] - hop[0, 0, 0] - sigma_in[:, 0, 0]
    base_imag = identity * ETA - hop[0, 0, 1] - sigma_in[:, 0, 1]

    def hosts(turn):
        found = []
        for r in range(rows):
            for k in range(mom_count):
                for e in range(e_local):
                    x = e_local * k + e
                    found.append((r * ROW + x, r * ROW + (x - turn) % ROW, k))
        return found

    def bundle_for(e):
        return jnp.stack(
            [
                lax.dynamic_index_in_dim(base_real, e, 0, False),
                lax.dynamic_index_in_dim(base_imag, e, 0, False),
                couple[0, 0, 0],
                couple[0, 0, 1],
            ]
        )

    parts = []
    for turn in range(ROW):
        target = lax.rem(place + turn, ROW)
        bundle = bundle_for(jnp.clip(target - e_local * mom, 0, e_local - 1))
        if turn:
            pairs = [(s * mom_count + k, h * mom_count + k) for h, s, k in hosts(turn)]
            bundle = lax.ppermute(bundle, ("slab", "mom"), pairs)
        parts.append(bundle)
    bundles = jnp.stack(parts)
    is_host = place // e_local == mom
    where = place[None]
    block = (2, width, width)
    green = jnp.zeros((ROW,) + block, jnp.float32)
    full = green
    received = jnp.zeros(block, jnp.float32)
    for r in range(rows):
        if r:
            pairs = [((r - 1) * ROW + x, r * ROW + x) for x in range(ROW)]
            received = lax.ppermute(green[ROW - 1], "slab", pairs)
        green = lax.cond(
            jnp.logical_and(is_host, row == r),
            lambda got: call(forward_kernel, [(ROW,) + block], (where, got, bundles))[0],
            lambda got: green,
            received,
        )
    received = jnp.zeros(block, jnp.float32)
    coupled = received
    for r in range(rows - 1, -1, -1):
        if r < rows - 1:
            pairs = [((r + 1) * ROW + x, r * ROW + x) for x in range(ROW)]
            received = lax.ppermute(coupled, "slab", pairs)
        full, coupled = lax.cond(
            jnp.logical_and(is_host, row == r),
            lambda got: tuple(call(backward_kernel, [(ROW,) + block, block], (where, got, bundles, green))),
            lambda got: (full, coupled),
            received,
        )
    mine = lax.dynamic_index_in_dim(full, place, 0, False)
    energy_at = place - e_local * mom
    blocks = [jnp.where(energy_at == e, mine, 0.0) for e in range(e_local)]
    for turn in range(1, ROW):
        pairs = [(h * mom_count + k, s * mom_count + k) for h, s, k in hosts(turn)]
        piece = lax.dynamic_index_in_dim(full, lax.rem(place - turn + ROW, ROW), 0, False)
        piece = lax.ppermute(piece, ("slab", "mom"), pairs)
        energy_at = lax.rem(place + turn, ROW) - e_local * mom
        blocks = [jnp.where(energy_at == e, piece, blocks[e]) for e in range(e_local)]
    own = jnp.stack(blocks)[:, None]
    phonon = phonon_matrix(shifts, mode_weight, total)
    mixed = jnp.einsum(
        "ef,fsrjl->esrjl",
        phonon,
        lax.all_to_all(own, "energy", split_axis=3, concat_axis=0, tiled=True),
        precision=HIGH,
    )
    return lax.psum(mixed, "mom") / mom_count


def solution(mesh):
    in_specs = (
        P("mom", "slab", None),
        P("mom", "slab", None, None, None),
        P("mom", "slab", None, None, None),
        P("energy", "slab", None, None, None),
        P(),
        P(),
    )
    out_specs = P(None, "slab", None, "energy", None)
    return jax.shard_map(body, mesh=mesh, in_specs=in_specs, out_specs=out_specs, check_vma=False)
```

time: 1810 us -> 335 us (0.19)
  waiting for transfers between devices: 1230 us -> 267 us
  starting transfers between devices: 464 us -> 30.3 us
  local copies, waits for them, and re-layouts: 72.4 us -> 9.88 us
  matrix products: 29.4 us -> 1.98 us
    ppermute x32 -> x12, waiting for transfers between devices: 1140 us -> 214 us  [the longest x3 149 us: body(): piece = lax.ppermute(piece, ('slab', 'mom'), pairs)]
    ppermute x32 -> x12, starting transfers between devices: 455 us -> 22.3 us  [the longest x3 11.6 us: body(): bundle = lax.ppermute(bundle, ('slab', 'mom'), pairs)]
    psum x1, waiting for transfers between devices: 66.7 us -> 29.2 us  [body(): return lax.psum(mixed, 'mom') / mom_count]
    sub x2 -> x1, local copies, waits for them, and re-layouts: 33 us -> 0.97 us  [body(): base_real = identity * z_real[:, None, :] - hop[0, 0, 0] - sigma_in[:, 0, 0]]
    dot_general x33 -> x1, matrix products: 29.4 us -> 1.98 us  [body(): jnp.einsum('ef,fsrjl->esrjl', phonon, lax.all_to_all(own, 'energy', split...]
    while x17 -> x0, local copies, waits for them, and re-layouts: 24.2 us -> none
  transfers between devices with their start and end apart: 34 -> 14, of which waited for: 34 -> 8; matrix products, arithmetic and copies ran while one was open for 0% -> 0% of each run, Pallas kernels for 0% -> 0%
where the time goes in v1:
time: 335 us; the launch traced here: 334 us
  waiting for transfers between devices  267 us (80%)
  starting transfers between devices  30.3 us (9%)
  between operations  13.9 us (4%)
  other arithmetic  11.7 us (3%)
  local copies, waits for them, and re-layouts  9.88 us (3%)
    ppermute x3, waiting for transfers between devices, body(): piece = lax.ppermute(piece, ('slab', 'mom'), pairs)  149 us
    ppermute x3, waiting for transfers between devices, body(): received = lax.ppermute(coupled, 'slab', pairs)  39.9 us
    psum x1, waiting for transfers between devices, body(): return lax.psum(mixed, 'mom') / mom_count  29.2 us
    all_to_all x1, waiting for transfers between devices, body(): lax.all_to_all(own, 'energy', split_axis=3, concat_axis=0, tiled=True)  23.6 us
    ppermute x3, waiting for transfers between devices, body(): bundle = lax.ppermute(bundle, ('slab', 'mom'), pairs)  18.8 us
    ppermute x3, starting transfers between devices, body(): bundle = lax.ppermute(bundle, ('slab', 'mom'), pairs)  11.6 us
    all_to_all x1, starting transfers between devices, body(): lax.all_to_all(own, 'energy', split_axis=3, concat_axis=0, tiled=True)  7.93 us
  transfers between devices with their start and end apart: 14, of which 8 were waited for; matrix products, arithmetic and copies ran while one was open for 0% of the time, Pallas kernels for 0%

profile of v1, /device:TPU:1, one launch (start us, length us, event | category | flops | bytes accessed | tf_op | source)
XLA Modules:
  0.0 334.4 jit_solution(4470317979571268295)
XLA Ops:
  6.6 1.1 bitcast_subtract_fusion.2
  7.6 1.0 slice_bitcast_fusion.5
  8.7 1.1 slice_bitcast_fusion.4
  9.8 0.1 broadcast_subtract_fusion
  9.8 0.1 bitcast_subtract_fusion.1
  10.0 0.2 constant_dynamic-slice_fusion.10
  10.2 1.4 fusion
  11.6 1.6 collective-permute-start
  13.2 7.7 %collective-permute-start.1 = (f32[4,256,256]{2,1,0:T(8,128)S(1)}, f32[4,256,256]{2,1,0:T(8,128)}, u32[]{:S(2)}, u32[]{:S(2)}) collective-permute-start(f32[4,256,256]{2,1,0:T(8,128)S(1)} %get-tuple-element.138), channel_id=1, source_target_pairs={{32,0},{48,16},{1,33},{17,49},{96,64},{112,80},{65,97},{81,113},{1... | collective-permute-start | bytes 3145736 | tf_op jit(solution)/shard_map/ppermute | solution.py:160
  20.9 2.3 collective-permute-start.2
  23.2 16.9 %collective-permute-done.1 = f32[4,256,256]{2,1,0:T(8,128)} collective-permute-done((f32[4,256,256]{2,1,0:T(8,128)S(1)}, f32[4,256,256]{2,1,0:T(8,128)}, u32[]{:S(2)}, u32[]{:S(2)}) %collective-permute-start.1) | collective-permute-done | bytes 1048608 | tf_op jit(solution)/shard_map/ppermute | solution.py:160
  40.1 1.8 collective-permute-done.2
  41.9 4.2 %pad_maximum_fusion = f32[4,4,256,256]{3,2,1,0:T(8,128)} fusion(f32[1,4,256,256]{3,2,1,0:T(8,128)} %bitcast.15, f32[1,4,256,256]{3,2,1,0:T(8,128)} %bitcast.14, f32[1,4,256,256]{3,2,1,0:T(8,128)} %bitcast.13, f32[1,4,256,256]{3,2,1,0:T(8,128)S(1)} %get-tuple-element.136), kind=kLoop, calls=%fused_computation | loop fusion | flops 3145728 | bytes 8388608 | tf_op jit(solution)/shard_map/stack | solution.py:162
  46.2 0.2 conditional.8
  46.2 0.2 broadcast_in_dim.5
  46.4 3.4 %collective-permute-start.3 = (f32[2,256,256]{2,1,0:T(8,128)S(1)}, f32[2,256,256]{2,1,0:T(8,128)S(1)}, u32[]{:S(2)}, u32[]{:S(2)}) collective-permute-start(f32[2,256,256]{2,1,0:T(8,128)S(1)} %slice_bitcast_fusion.2), channel_id=1, source_target_pairs={{0,64},{16,80},{32,96},{48,112},{1,65},{17,81},{33,97},{49,113},{2... | collective-permute-start | bytes 1572872 | tf_op jit(solution)/shard_map/ppermute | solution.py:172
  49.8 6.1 %collective-permute-done.3 = f32[2,256,256]{2,1,0:T(8,128)S(1)} collective-permute-done((f32[2,256,256]{2,1,0:T(8,128)S(1)}, f32[2,256,256]{2,1,0:T(8,128)S(1)}, u32[]{:S(2)}, u32[]{:S(2)}) %collective-permute-start.3) | collective-permute-done | bytes 524320 | tf_op jit(solution)/shard_map/ppermute | solution.py:172
  55.9 0.7 collective-permute-start.4
  56.7 0.7 collective-permute-start.5
  57.4 1.8 conditional.12
  57.4 1.6 broadcast_in_dim.11
  59.2 0.7 collective-permute-start.6
  59.9 0.7 collective-permute-start.7
  60.7 1.3 collective-permute-start.8
  62.0 39.9 %collective-permute-done.8 = f32[2,256,256]{2,1,0:T(8,128)S(1)} collective-permute-done((f32[2,256,256]{2,1,0:T(8,128)S(1)}, f32[2,256,256]{2,1,0:T(8,128)S(1)}, u32[]{:S(2)}, u32[]{:S(2)}) %collective-permute-start.8) | collective-permute-done | bytes 524320 | tf_op jit(solution)/shard_map/ppermute | solution.py:184
  101.9 1.7 constant_dynamic-slice_fusion
  103.6 0.4 copy.41
  104.0 1.3 collective-permute-start.10
  105.3 0.4 copy.40
  105.7 0.7 collective-permute-start.11
  106.4 0.4 copy.42
  106.8 1.3 collective-permute-start.9
  108.2 143.3 %collective-permute-done.10 = f32[2,256,256]{2,0,1:T(2,128)S(1)} collective-permute-done((f32[2,256,256]{2,0,1:T(2,128)S(1)}, f32[2,256,256]{2,0,1:T(2,128)S(1)}, u32[]{:S(2)}, u32[]{:S(2)}) %collective-permute-start.10) | collective-permute-done | bytes 524320 | tf_op jit(solution)/shard_map/ppermute | solution.py:197
  251.5 5.7 %collective-permute-done.9 = f32[2,256,256]{2,0,1:T(2,128)} collective-permute-done((f32[2,256,256]{2,0,1:T(2,128)S(1)}, f32[2,256,256]{2,0,1:T(2,128)}, u32[]{:S(2)}, u32[]{:S(2)}) %collective-permute-start.9) | collective-permute-done | bytes 524320 | tf_op jit(solution)/shard_map/ppermute | solution.py:197
  257.1 1.9 fusion.6
  259.0 1.4 maximum_bitcast_fusion
  260.5 7.9 %all-to-all-start = ((f32[2,1,2,256,256]{4,2,0,1,3:T(2,128)}), f32[2,1,2,256,256]{4,2,0,1,3:T(2,128)S(1)}, u32[]{:S(2)}, u32[]{:S(2)}) async-start(f32[2,1,2,256,256]{4,2,0,1,3:T(2,128)} %maximum_bitcast_fusion), calls=%async_computation | async-start | bytes 2097152 | tf_op jit(solution)/shard_map/all_to_all | solution.py:205
  268.4 0.0 all-reduce.2.cloned.1.call-start
  268.5 0.1 iota_add_fusion
  268.5 0.1 add_reduce_fusion
  268.6 23.6 %all-to-all-done = f32[2,1,2,256,256]{4,2,0,1,3:T(2,128)S(1)} async-done(((f32[2,1,2,256,256]{4,2,0,1,3:T(2,128)}), f32[2,1,2,256,256]{4,2,0,1,3:T(2,128)S(1)}, u32[]{:S(2)}, u32[]{:S(2)}) %all-to-all-start) | async-done | bytes 1048608 | tf_op jit(solution)/shard_map/all_to_all | solution.py:205
  292.2 0.5 copy.39
  292.8 0.7 reshape.104
  293.5 2.0 convolution_bitcast_fusion
  295.5 0.0 all-reduce.2.cloned.1.call-update
  295.5 29.2 %all-reduce.2.cloned.1.call-done = f32[16,1,2,32,256]{4,0,3,2,1:T(8,128)} async-done(((f32[16,1,2,32,256]{4,0,3,2,1:T(8,128)}), f32[16,1,2,32,256]{4,0,3,2,1:T(8,128)}) %all-reduce.2.cloned.1.call-update) | async-done | bytes 1048592 | tf_op jit(solution)/shard_map/psum | solution.py:208
  324.7 1.3 broadcast_multiply_fusion
  326.0 1.6 copy.28
  (27 shorter events, 0.2 us)
Async XLA Ops:
  6.5 3.2 copy-start.1
  6.5 3.3 copy-start
  11.6 11.6 %collective-permute-start = (f32[4,256,256]{2,1,0:T(8,128)}, f32[4,256,256]{2,1,0:T(8,128)}, u32[]{:S(2)}, u32[]{:S(2)}) collective-permute-start(f32[4,256,256]{2,1,0:T(8,128)} %get-tuple-element.137), channel_id=1, source_target_pairs={{48,0},{0,16},{17,33},{33,49},{112,64},{64,80},{81,97},{97,113},{1... | collective-permute-start | bytes 3145736 | tf_op jit(solution)/shard_map/ppermute | solution.py:160
  13.2 26.9 %collective-permute-start.1 = (f32[4,256,256]{2,1,0:T(8,128)S(1)}, f32[4,256,256]{2,1,0:T(8,128)}, u32[]{:S(2)}, u32[]{:S(2)}) collective-permute-start(f32[4,256,256]{2,1,0:T(8,128)S(1)} %get-tuple-element.138), channel_id=1, source_target_pairs={{32,0},{48,16},{1,33},{17,49},{96,64},{112,80},{65,97},{81,113},{1... | collective-permute-start | bytes 3145736 | tf_op jit(solution)/shard_map/ppermute | solution.py:160
  20.9 21.0 %collective-permute-start.2 = (f32[4,256,256]{2,1,0:T(8,128)S(1)}, f32[4,256,256]{2,1,0:T(8,128)}, u32[]{:S(2)}, u32[]{:S(2)}) collective-permute-start(f32[4,256,256]{2,1,0:T(8,128)S(1)} %get-tuple-element.139), channel_id=1, source_target_pairs={{16,0},{32,16},{49,33},{1,49},{80,64},{96,80},{113,97},{65,113},{1... | collective-permute-start | bytes 3145736 | tf_op jit(solution)/shard_map/ppermute | solution.py:160
  46.4 9.4 %collective-permute-start.3 = (f32[2,256,256]{2,1,0:T(8,128)S(1)}, f32[2,256,256]{2,1,0:T(8,128)S(1)}, u32[]{:S(2)}, u32[]{:S(2)}) collective-permute-start(f32[2,256,256]{2,1,0:T(8,128)S(1)} %slice_bitcast_fusion.2), channel_id=1, source_target_pairs={{0,64},{16,80},{32,96},{48,112},{1,65},{17,81},{33,97},{49,113},{2... | collective-permute-start | bytes 1572872 | tf_op jit(solution)/shard_map/ppermute | solution.py:172
  55.9 0.7 collective-permute-start.4
  56.7 0.7 collective-permute-start.5
  59.2 0.7 collective-permute-start.6
  59.9 0.7 collective-permute-start.7
  60.7 41.3 %collective-permute-start.8 = (f32[2,256,256]{2,1,0:T(8,128)S(1)}, f32[2,256,256]{2,1,0:T(8,128)S(1)}, u32[]{:S(2)}, u32[]{:S(2)}) collective-permute-start(f32[2,256,256]{2,1,0:T(8,128)S(1)} %get-tuple-element.127), channel_id=1, source_target_pairs={{64,0},{80,16},{96,32},{112,48},{65,1},{81,17},{97,33},{113,49},{6... | collective-permute-start | bytes 1572872 | tf_op jit(solution)/shard_map/ppermute | solution.py:184
  104.0 147.5 %collective-permute-start.10 = (f32[2,256,256]{2,0,1:T(2,128)S(1)}, f32[2,256,256]{2,0,1:T(2,128)S(1)}, u32[]{:S(2)}, u32[]{:S(2)}) collective-permute-start(f32[2,256,256]{2,0,1:T(2,128)S(1)} %bitcast.82), channel_id=1, source_target_pairs={{0,32},{16,48},{33,1},{49,17},{64,96},{80,112},{97,65},{113,81},{1... | collective-permute-start | bytes 1572872 | tf_op jit(solution)/shard_map/ppermute | solution.py:197
  105.7 145.7 %collective-permute-start.11 = (f32[2,256,256]{2,0,1:T(2,128)S(1)}, f32[2,256,256]{2,0,1:T(2,128)S(1)}, u32[]{:S(2)}, u32[]{:S(2)}) collective-permute-start(f32[2,256,256]{2,0,1:T(2,128)S(1)} %bitcast.83), channel_id=1, source_target_pairs={{0,48},{16,0},{33,17},{49,33},{64,112},{80,64},{97,81},{113,97},{1... | collective-permute-start | bytes 1572872 | tf_op jit(solution)/shard_map/ppermute | solution.py:197
  106.8 150.3 %collective-permute-start.9 = (f32[2,256,256]{2,0,1:T(2,128)S(1)}, f32[2,256,256]{2,0,1:T(2,128)}, u32[]{:S(2)}, u32[]{:S(2)}) collective-permute-start(f32[2,256,256]{2,0,1:T(2,128)S(1)} %bitcast.84), channel_id=1, source_target_pairs={{0,16},{16,32},{33,49},{49,1},{64,80},{80,96},{97,113},{113,65},{1... | collective-permute-start | bytes 1572872 | tf_op jit(solution)/shard_map/ppermute | solution.py:197
  259.0 9.4 %copy-start.2 = (f32[2,4]{1,0:T(2,128)S(1)}, f32[2,4]{1,0:T(2,128)}, u32[]{:S(2)}) copy-start(f32[2,4]{1,0:T(2,128)} %param.27) | copy-start | bytes 100
  259.0 9.4 %copy-start.3 = (s32[4]{0:T(128)S(1)}, s32[4]{0:T(128)}, u32[]{:S(2)}) copy-start(s32[4]{0:T(128)} %param.26) | copy-start | bytes 52
  260.5 31.8 %all-to-all-start = ((f32[2,1,2,256,256]{4,2,0,1,3:T(2,128)}), f32[2,1,2,256,256]{4,2,0,1,3:T(2,128)S(1)}, u32[]{:S(2)}, u32[]{:S(2)}) async-start(f32[2,1,2,256,256]{4,2,0,1,3:T(2,128)} %maximum_bitcast_fusion), calls=%async_computation | async-start | bytes 2097152 | tf_op jit(solution)/shard_map/all_to_all | solution.py:205
  268.4 56.3 %all-reduce.2.cloned.1.call-start = ((), (), s32[]{:S(2)}) async-start(), calls=%async_computation.1 | async-start | bytes 2097152 | tf_op jit(solution)/shard_map/psum | solution.py:208
Sparse Core Ops, SparseCore 0:
  295.6 29.0 all-reduce.1

commit v2 on v0

v2 whole, which is shorter than its diff:
```python
import functools

import jax
import jax.numpy as jnp
from jax import lax
from jax.experimental import pallas as pl
from jax.experimental.pallas import tpu as pltpu
from jax.sharding import PartitionSpec as P

ETA = 0.5
ROW = 4
MESH = pl.DeviceIdType.MESH


def split(mat):
    top = mat.astype(jnp.bfloat16)
    return top, (mat - top.astype(jnp.float32)).astype(jnp.bfloat16)


def prep(pair):
    return split(pair[0]), split(pair[1]), split(pair[0] + pair[1])


def prep_adjoint(pair):
    return prep((pair[0].T, -pair[1].T))


def mul(left, right):
    outs = []
    for (left_top, left_low), (top, low) in zip(left, right):
        outs.append(
            jnp.dot(
                jnp.concatenate([left_top, left_top, left_low], axis=1),
                jnp.concatenate([top, low, top], axis=0),
                preferred_element_type=jnp.float32,
            )
        )
    return outs[0] - outs[1], outs[2] - (outs[0] + outs[1])


def eye_mask(size):
    shape = (size, size)
    return lax.broadcasted_iota(jnp.int32, shape, 0) == lax.broadcasted_iota(jnp.int32, shape, 1)


def on_diagonal(mat, change):
    half = mat.shape[0] // 2
    upper = jnp.concatenate([change(mat[:half, :half], 0), mat[:half, half:]], axis=1)
    lower = jnp.concatenate([mat[half:, :half], change(mat[half:, half:], 1)], axis=1)
    return jnp.concatenate([upper, lower], axis=0)


def newton_inverse(mat):
    half = mat[0].shape[0] // 2
    eye = eye_mask(half)
    blocks = [
        [jnp.where(eye, part[:half, :half], 0.0), jnp.where(eye, part[half:, half:], 0.0)]
        for part in mat
    ]

    def inverse(diag):
        scale = 1.0 / (diag[0] * diag[0] + diag[1] * diag[1])
        return diag[0] * scale, -diag[1] * scale

    row = inverse(
        [jnp.concatenate([jnp.sum(b, axis=0, keepdims=True) for b in pair], axis=1) for pair in blocks]
    )
    col = inverse(
        [jnp.concatenate([jnp.sum(b, axis=1, keepdims=True) for b in pair], axis=0) for pair in blocks]
    )
    off = [on_diagonal(part, lambda block, n: jnp.where(eye, 0.0, block)) for part in mat]
    first = (off[0] * row[0] - off[1] * row[1], off[0] * row[1] + off[1] * row[0])
    fixed = prep(first)
    second = mul(fixed, fixed)
    third = mul(prep(second), fixed)
    real = second[0] - first[0] - third[0]
    imag = second[1] - first[1] - third[1]
    real = on_diagonal(real, lambda block, n: block + jnp.where(eye, 1.0, 0.0))
    return col[0] * real - col[1] * imag, col[0] * imag + col[1] * real


def load(ref):
    return ref[0], ref[1]


def store(ref, pair):
    ref[0] = pair[0]
    ref[1] = pair[1]


def kernel(
    rows, depth, e_local,
    mix, levels, hop, couple, sigma, out,
    outgoing, base, coup, green, left, h_coup, h_green, h_adj, h_first, h_second,
    h_chain, chain, full, gathered, summed, mixed,
    s_base, r_base, s_coup, r_coup, s_hcoup, r_hcoup, s_hgreen, r_hgreen,
    s_hop, r_hop, s_chain, r_chain, s_back, r_back, s_first, r_first,
    s_second, r_second, s_last, r_last,
):
    slab = lax.axis_index("slab")
    plane = lax.axis_index("energy")
    mom = lax.axis_index("mom")
    y, x = slab // ROW, lax.rem(slab, ROW)
    other = 1 - mom
    width = hop.shape[-1]
    share = width // depth
    is_main = x // e_local == mom
    at_start = jnp.logical_and(y == 0, x == 0)

    def send(src, dst, send_sem, recv_sem, **where):
        return pltpu.make_async_remote_copy(
            src_ref=src, dst_ref=dst, send_sem=send_sem, recv_sem=recv_sem,
            device_id=where, device_id_type=MESH,
        )

    def arrived(dst, recv_sem):
        send(dst, dst, s_hop.at[0], recv_sem, mom=other).wait_recv()

    barrier = pltpu.get_barrier_semaphore()

    def greet(**where):
        pl.semaphore_signal(barrier, inc=1, device_id=where, device_id_type=MESH)

    greet(mom=other)
    for turn in range(1, ROW):
        peer = y * ROW + lax.rem(x + turn, ROW)
        greet(slab=peer, mom=mom)
        greet(slab=peer, mom=other)
    for turn in (1, rows - 1):
        greet(slab=lax.rem(y + turn, rows) * ROW + x)
    for turn in range(1, depth):
        greet(energy=lax.rem(plane + turn, depth))
    pl.semaphore_wait(barrier, 1 + 2 * (ROW - 1) + 2 + depth - 1)

    half = width // 2
    eye = eye_mask(half)

    def base_copy(e):
        return send(
            outgoing.at[e], base.at[x], s_base.at[e], r_base.at[x], slab=y * ROW + e_local * mom + e
        )

    def coup_copy(e):
        return send(couple, coup.at[x], s_coup.at[e], r_coup.at[x], slab=y * ROW + e_local * mom + e)

    def is_remote(e):
        return e_local * mom + e != x

    def sends_coup(e):
        return jnp.logical_and(is_remote(e), jnp.logical_not(at_start))

    for e in range(e_local):
        level = levels[e : e + 1]
        real = on_diagonal(
            -hop[0] - sigma[e, 0],
            lambda block, n: block + jnp.where(eye, level[:, n * half : (n + 1) * half], 0.0),
        )
        imag = on_diagonal(
            -hop[1] - sigma[e, 1], lambda block, n: block + jnp.where(eye, ETA, 0.0)
        )

        @pl.when(is_remote(e))
        def _():
            store(outgoing.at[e], (real, imag))
            base_copy(e).start()

        @pl.when(jnp.logical_not(is_remote(e)))
        def _():
            store(base.at[x], (real, imag))
            store(coup.at[x], load(couple))

    for e in range(e_local):

        @pl.when(sends_coup(e))
        def _():
            coup_copy(e).start()

    def hcoup_copy(j):
        return send(coup.at[j], h_coup.at[j], s_hcoup.at[j], r_hcoup.at[j], mom=other)

    def hgreen_copy(j):
        return send(green.at[j + 1], h_green.at[j], s_hgreen.at[j], r_hgreen.at[j], mom=other)

    def hop_copy():
        return send(green.at[ROW], green.at[0], s_hop.at[0], r_hop.at[0], slab=slab + ROW)

    def chain_copy(j):
        return send(h_chain.at[j + 1], chain.at[j], s_chain.at[j], r_chain.at[j], mom=other)

    def back_copy():
        return send(h_chain.at[0], h_chain.at[ROW], s_back.at[0], r_back.at[0], slab=slab - ROW)

    def first_copy(j, part):
        return send(
            full.at[j, part], gathered.at[x], s_first.at[j, part], r_first.at[x],
            slab=y * ROW + j, mom=part,
        )

    def is_first(j):
        return jnp.logical_and(y == 0, j == 0)

    def is_last(j):
        return jnp.logical_and(y == rows - 1, j == ROW - 1)

    def first_remote(j, part):
        return jnp.logical_or(j != x, part != mom)

    @pl.when(is_main)
    def _():
        @pl.when(y > 0)
        def _():
            arrived(green.at[0], r_hop.at[0])

        def forward(j, carry):
            @pl.when(j != x)
            def _():
                arrived(base.at[j], r_base.at[j])

            @pl.when(is_first(j))
            def _():
                left[...] = jnp.zeros_like(left)

            @pl.when(jnp.logical_not(is_first(j)))
            def _():
                @pl.when(j != x)
                def _():
                    arrived(coup.at[j], r_coup.at[j])

                hcoup_copy(j).start()
                coupling = load(coup.at[j])
                half_way = mul(prep(load(green.at[j])), prep_adjoint(coupling))
                store(left, mul(prep(coupling), prep(half_way)))

            store(
                green.at[j + 1],
                newton_inverse((base[j, 0] - left[0], base[j, 1] - left[1])),
            )

            @pl.when(jnp.logical_not(is_first(j)))
            def _():
                hgreen_copy(j).start()

            return carry

        lax.fori_loop(0, ROW, forward, 0)

        @pl.when(y < rows - 1)
        def _():
            hop_copy().start()

        def backward(turn, carry):
            j = ROW - 1 - turn

            @pl.when(is_last(j))
            def _():
                full[j] = green[j + 1]

            @pl.when(jnp.logical_not(is_last(j)))
            def _():
                arrived(chain.at[j], r_chain.at[j])
                pair = load(green.at[j + 1])
                ready = prep(pair)
                extra = mul(prep(mul(ready, prep(load(chain.at[j])))), ready)
                store(full.at[j], (pair[0] + extra[0], pair[1] + extra[1]))

            for part in range(2):

                @pl.when(first_remote(j, part))
                def _():
                    first_copy(j, part).start()

                @pl.when(jnp.logical_not(first_remote(j, part)))
                def _():
                    gathered[x] = full[j, part]

            return carry

        lax.fori_loop(0, ROW, backward, 0)

    @pl.when(jnp.logical_not(is_main))
    def _():
        def forward(j, carry):
            @pl.when(jnp.logical_not(is_first(j)))
            def _():
                arrived(h_coup.at[j], r_hcoup.at[j])
                coupling = load(h_coup.at[j])
                adjoint = (coupling[0].T, -coupling[1].T)
                store(h_adj.at[j], adjoint)
                arrived(h_green.at[j], r_hgreen.at[j])
                ready = prep(load(h_green.at[j]))
                store(h_first.at[j], mul(prep(adjoint), ready))
                store(h_second.at[j], mul(ready, prep(coupling)))

            return carry

        lax.fori_loop(0, ROW, forward, 0)

        @pl.when(y == rows - 1)
        def _():
            h_chain[ROW] = jnp.zeros_like(h_chain.at[ROW])

        @pl.when(y < rows - 1)
        def _():
            arrived(h_chain.at[ROW], r_back.at[0])

        def backward(turn, carry):
            j = ROW - 1 - turn

            @pl.when(jnp.logical_not(is_last(j)))
            def _():
                chain_copy(j).start()

            @pl.when(jnp.logical_not(is_first(j)))
            def _():
                extra = mul(prep(load(h_first.at[j])), prep(load(h_chain.at[j + 1])))
                adjoint = load(h_adj.at[j])
                sums = (adjoint[0] + extra[0], adjoint[1] + extra[1])
                store(h_chain.at[j], mul(prep(sums), prep(load(h_second.at[j]))))

            return carry

        lax.fori_loop(0, ROW, backward, 0)

        @pl.when(y > 0)
        def _():
            back_copy().start()

    for c in range(ROW):

        @pl.when(jnp.logical_or(c != x, jnp.logical_not(is_main)))
        def _():
            arrived(gathered.at[c], r_first.at[c])

    for e in range(e_local):
        summed[e] = gathered[e] + gathered[e_local + e]

    def second_copy(turn):
        target = lax.rem(plane + turn, depth)
        return send(
            summed.at[:, pl.ds(pl.multiple_of(target * share, 8), share)], mixed.at[plane],
            s_second.at[turn], r_second.at[plane], energy=target,
        )

    for turn in range(1, depth):
        second_copy(turn).start()
    mixed[plane] = summed[:, pl.ds(pl.multiple_of(plane * share, 8), share)]
    for turn in range(1, depth):
        source = lax.rem(plane + turn, depth)
        arrived(mixed.at[source], r_second.at[source])

    def mixing(e, carry):
        total = jnp.zeros((share, width), jnp.float32)
        for f in range(depth * e_local):
            total = total + mix[e, f] * mixed[f // e_local, f % e_local]
        out[e, mom] = total
        return carry

    lax.fori_loop(0, depth * e_local, mixing, 0)
    last_copy = send(out.at[:, mom], out.at[:, mom], s_last.at[0], r_last.at[0], mom=other)
    last_copy.start()

    for e in range(e_local):

        @pl.when(is_remote(e))
        def _():
            base_copy(e).wait_send()

        @pl.when(sends_coup(e))
        def _():
            coup_copy(e).wait_send()

    @pl.when(is_main)
    def _():
        for j in range(ROW):

            @pl.when(jnp.logical_not(is_first(j)))
            def _():
                hcoup_copy(j).wait_send()
                hgreen_copy(j).wait_send()

            for part in range(2):

                @pl.when(first_remote(j, part))
                def _():
                    first_copy(j, part).wait_send()

        @pl.when(y < rows - 1)
        def _():
            hop_copy().wait_send()

    @pl.when(jnp.logical_not(is_main))
    def _():
        for j in range(ROW):

            @pl.when(jnp.logical_not(is_last(j)))
            def _():
                chain_copy(j).wait_send()

        @pl.when(y > 0)
        def _():
            back_copy().wait_send()

    for turn in range(1, depth):
        second_copy(turn).wait_send()
    last_copy.wait_send()
    arrived(out.at[:, other], r_last.at[0])


def phonon_matrix(shifts, mode_weight, count):
    rows = jnp.arange(count)[:, None, None]
    cols = jnp.arange(count)[None, :, None]
    offset = shifts[None, None, :]
    upper = (cols == rows + offset).astype(jnp.float32)
    lower = (cols == rows - offset).astype(jnp.float32)
    return jnp.sum(upper * mode_weight[0] + lower * mode_weight[1], axis=2)


def body(onsite, hop, couple, sigma_in, shifts, mode_weight):
    e_local = sigma_in.shape[0]
    width = onsite.shape[-1]
    rows = lax.axis_size("slab") // ROW
    depth = lax.axis_size("energy")
    mom_count = lax.axis_size("mom")
    total = e_local * depth
    share = width // depth
    global_index = lax.axis_index("energy") * e_local + jnp.arange(e_local)
    energies = -0.5 + (global_index.astype(jnp.float32) + 0.5) / total
    levels = energies[:, None] - onsite[0, 0][None, :]
    mix = phonon_matrix(shifts, mode_weight, total) / mom_count
    block = (2, width, width)

    def buffer(*shape):
        return pltpu.VMEM(shape, jnp.float32)

    def sems(*shape):
        return pltpu.SemaphoreType.DMA(shape)

    vmem = pl.BlockSpec(memory_space=pltpu.VMEM)
    result = pl.pallas_call(
        functools.partial(kernel, rows, depth, e_local),
        out_shape=jax.ShapeDtypeStruct((total, 2, share, width), jnp.float32),
        in_specs=[pl.BlockSpec(memory_space=pltpu.SMEM)] + [vmem] * 4,
        out_specs=vmem,
        scratch_shapes=[
            buffer(e_local, *block),
            buffer(ROW, *block),
            buffer(ROW, *block),
            buffer(ROW + 1, *block),
            buffer(*block),
            buffer(ROW, *block),
            buffer(ROW, *block),
            buffer(ROW, *block),
            buffer(ROW, *block),
            buffer(ROW, *block),
            buffer(ROW + 1, *block),
            buffer(ROW, *block),
            buffer(ROW, *block),
            buffer(ROW, width, width),
            buffer(e_local, width, width),
            buffer(depth, e_local, share, width),
            sems(e_local), sems(ROW), sems(e_local), sems(ROW),
            sems(ROW), sems(ROW), sems(ROW), sems(ROW),
            sems(1), sems(1), sems(ROW), sems(ROW), sems(1), sems(1),
            sems(ROW, 2), sems(ROW), sems(depth), sems(depth), sems(1), sems(1),
        ],
        compiler_params=pltpu.CompilerParams(
            collective_id=0, has_side_effects=True, vmem_limit_bytes=56 << 20
        ),
    )(mix, levels, hop[0, 0], couple[0, 0], sigma_in[:, 0])
    return result[:, None]


def solution(mesh):
    in_specs = (
        P("mom", "slab", None),
        P("mom", "slab", None, None, None),
        P("mom", "slab", None, None, None),
        P("energy", "slab", None, None, None),
        P(),
        P(),
    )
    out_specs = P(None, "slab", None, "energy", None)
    return jax.shard_map(body, mesh=mesh, in_specs=in_specs, out_specs=out_specs, check_vma=False)
```

time: 1810 us -> 164 us (0.09)
  waiting for transfers between devices: 1230 us -> 0 us
  starting transfers between devices: 464 us -> 0 us
  Pallas kernels: 0 us -> 159 us
  local copies, waits for them, and re-layouts: 72.4 us -> 3.68 us
  matrix products: 29.4 us -> 0 us
    ppermute x32 -> x0, waiting for transfers between devices: 1140 us -> none  [shifted(): return lax.ppermute(shard, axis, pairs)]
    ppermute x32 -> x0, starting transfers between devices: 455 us -> none  [shifted(): return lax.ppermute(shard, axis, pairs)]
    pallas_call x0 -> x1, Pallas kernels: none -> 159 us  [body(): pl.pallas_call(functools.partial(kernel, rows, depth, e_local), out_shape...]
    psum x1 -> x0, waiting for transfers between devices: 66.7 us -> none  [body(): result = lax.psum(mixed, 'mom') / mom_count]
    sub x2 -> x0, local copies, waits for them, and re-layouts: 33 us -> none  [the longest x1 16.5 us: forward(): mat_imag = identity * ETA - hopping[1] - sig[:, 1] - left[1]]
    dot_general x33 -> x0, matrix products: 29.4 us -> none  [the longest x32 27.4 us: product(): return jnp.einsum(form, first, second, precision=HIGH)]
    while x17 -> x0, local copies, waits for them, and re-layouts: 24.2 us -> none
  transfers between devices with their start and end apart: 34 -> 0, of which waited for: 34 -> 0; matrix products, arithmetic and copies ran while one was open for 0% -> 0% of each run, Pallas kernels for 0% -> 0%
where the time goes in v2:
time: 164 us
  Pallas kernels  159 us (97%)
  local copies, waits for them, and re-layouts  3.68 us (2%)
    pallas_call x1, Pallas kernels, body(): pl.pallas_call(functools.partial(kernel, rows, depth, e_local), out_shape...  159 us
    unnamed x7, local copies, waits for them, and re-layouts  3.67 us

profile of v2, /device:TPU:1, one launch (start us, length us, event | category | flops | bytes accessed | tf_op | source)
XLA Modules:
  0.0 163.8 jit_solution(12640124094739118206)
XLA Ops:
  0.0 0.0 copy-start.1
  0.0 0.7 copy-done.1
  0.7 0.0 copy-start
  0.7 0.7 copy-done
  1.4 0.0 copy-start.2
  1.4 0.6 broadcast_subtract_fusion.levels
  2.0 0.0 copy-done.2
  2.0 0.1 iota_add_fusion
  2.1 0.1 add_reduce_fusion
  2.2 0.6 broadcast_multiply_fusion.mix
  2.8 158.7 %shard_map.64 = f32[16,2,32,256]{3,2,1,0:T(8,128)} custom-call(f32[16,16]{1,0:T(8,128)} %broadcast_multiply_fusion.mix, f32[2,256]{1,0:T(2,128)} %broadcast_subtract_fusion.levels, f32[2,256,256]{2,1,0:T(8,128)} %bitcast.13, f32[2,256,256]{2,1,0:T(8,128)} %bitcast.14, f32[2,2,256,256]{3,2,1,0:T(8,128)} %bitcast.12), custom_call_target="tpu_custom_call" | custom-call | tf_op jit(solution)/shard_map/pallas_call | solution.py:439
  161.5 2.3 %copy.10 = f32[16,1,2,32,256]{4,3,2,1,0:T(8,128)} copy(f32[16,1,2,32,256]{4,3,2,1,0:T(8,128)} %bitcast.11) | data formatting | bytes 2097152
  (2 shorter events, 0.0 us)
Async XLA Ops:
  0.0 0.7 copy-start.1
  0.7 0.7 copy-start
  1.4 0.7 copy-start.2

commit v3 on v2

v3 whole, which is shorter than its diff:
```python
import functools

import jax
import jax.numpy as jnp
from jax import lax
from jax.experimental import pallas as pl
from jax.experimental.pallas import tpu as pltpu
from jax.sharding import PartitionSpec as P

ETA = 0.5
ROW = 4
CUT = 6
PIECES = 4
MESH = pl.DeviceIdType.MESH


def split(mat):
    top = mat.astype(jnp.bfloat16)
    return top, (mat - top.astype(jnp.float32)).astype(jnp.bfloat16)


def prep(pair):
    return split(pair[0]), split(pair[1]), split(pair[0] + pair[1])


def prep_adjoint(pair):
    return prep((pair[0].T, -pair[1].T))


def mul(left, right):
    outs = []
    for (left_top, left_low), (top, low) in zip(left, right):
        outs.append(
            jnp.dot(
                jnp.concatenate([left_top, left_top, left_low], axis=1),
                jnp.concatenate([top, low, top], axis=0),
                preferred_element_type=jnp.float32,
            )
        )
    return outs[0] - outs[1], outs[2] - (outs[0] + outs[1])


def eye_mask(size):
    shape = (size, size)
    return lax.broadcasted_iota(jnp.int32, shape, 0) == lax.broadcasted_iota(jnp.int32, shape, 1)


def on_diagonal(mat, change):
    half = mat.shape[0] // 2
    upper = jnp.concatenate([change(mat[:half, :half], 0), mat[:half, half:]], axis=1)
    lower = jnp.concatenate([mat[half:, :half], change(mat[half:, half:], 1)], axis=1)
    return jnp.concatenate([upper, lower], axis=0)


def newton_inverse(mat):
    half = mat[0].shape[0] // 2
    eye = eye_mask(half)
    blocks = [
        [jnp.where(eye, part[:half, :half], 0.0), jnp.where(eye, part[half:, half:], 0.0)]
        for part in mat
    ]

    def inverse(diag):
        scale = 1.0 / (diag[0] * diag[0] + diag[1] * diag[1])
        return diag[0] * scale, -diag[1] * scale

    row = inverse(
        [jnp.concatenate([jnp.sum(b, axis=0, keepdims=True) for b in pair], axis=1) for pair in blocks]
    )
    col = inverse(
        [jnp.concatenate([jnp.sum(b, axis=1, keepdims=True) for b in pair], axis=0) for pair in blocks]
    )
    off = [on_diagonal(part, lambda block, n: jnp.where(eye, 0.0, block)) for part in mat]
    first = (off[0] * row[0] - off[1] * row[1], off[0] * row[1] + off[1] * row[0])
    fixed = prep(first)
    second = mul(fixed, fixed)
    third = mul(prep(second), fixed)
    real = second[0] - first[0] - third[0]
    imag = second[1] - first[1] - third[1]
    real = on_diagonal(real, lambda block, n: block + jnp.where(eye, 1.0, 0.0))
    return col[0] * real - col[1] * imag, col[0] * imag + col[1] * real


def load(ref):
    return ref[0], ref[1]


def store(ref, pair):
    ref[0] = pair[0]
    ref[1] = pair[1]


def kernel(
    cut, slabs, depth, e_local,
    shifts, weights, onsite, hop_in, couple, sigma_in, out,
    hop, sigma, outgoing, left, box_a, box_b, box_c, box_d, box_e, gathered, summed, mixed, total,
    mix, s_in,
    s_base, r_base, s_coup, r_coup, s_hcoup, r_hcoup, s_hgreen, r_hgreen,
    s_hop, r_hop, s_chain, r_chain, s_back, r_back, s_first, r_first,
    s_second, r_second, s_last, r_last,
):
    base = h_coup = h_adj = box_a
    coup = h_green = h_first = box_b
    green = h_chain = box_c
    chain = h_second = box_d
    full = box_e
    slab = lax.axis_index("slab")
    plane = lax.axis_index("energy")
    mom = lax.axis_index("mom")
    y, x = slab // ROW, lax.rem(slab, ROW)
    other = 1 - mom
    width = hop.shape[-1]
    share = width // depth
    span = width // PIECES
    half = width // 2
    near, far = 0, 2 * ROW
    in_far = jnp.where(slab >= cut, 1, 0)
    host_row = jnp.where(slab >= cut, far, near)
    is_near, is_far = y == 0, y == 2
    is_host = jnp.logical_or(is_near, is_far)
    is_main = jnp.logical_and(is_host, x // e_local == mom)
    is_helper = jnp.logical_and(is_host, x // e_local != mom)
    at_start = slab == 0
    offset = jnp.where(is_near, 0, cut)
    count = jnp.where(is_near, cut, slabs - cut)

    def send(src, dst, send_sem, recv_sem, **where):
        return pltpu.make_async_remote_copy(
            src_ref=src, dst_ref=dst, send_sem=send_sem, recv_sem=recv_sem,
            device_id=where, device_id_type=MESH,
        )

    def arrived(dst, recv_sem):
        send(dst, dst, s_hop.at[0], recv_sem, mom=other).wait_recv()

    hop_load = pltpu.make_async_copy(hop_in, hop, s_in.at[0])
    sigma_load = pltpu.make_async_copy(sigma_in, sigma, s_in.at[1])
    hop_load.start()
    sigma_load.start()
    barrier = pltpu.get_barrier_semaphore()

    def greet(**where):
        pl.semaphore_signal(barrier, inc=1, device_id=where, device_id_type=MESH)

    def hosted_here():
        return jnp.logical_and(is_host, y * ROW == host_row)

    greet(mom=other)
    for turn in range(1, depth):
        greet(energy=lax.rem(plane + turn, depth))
    for c in range(ROW):

        @pl.when(host_row + c != slab)
        def _():
            greet(slab=host_row + c, mom=c // e_local)

    @pl.when(is_host)
    def _():
        greet(slab=far - y * ROW + x)

    @pl.when(is_main)
    def _():
        def call(j, carry):
            @pl.when(offset + j != slab)
            def _():
                greet(slab=offset + j, mom=mom)
                greet(slab=offset + j, mom=other)

            return carry

        lax.fori_loop(0, count, call, 0)

    expected = depth + ROW - jnp.where(hosted_here(), 1, 0) + jnp.where(is_host, 1, 0)
    pl.semaphore_wait(barrier, expected + jnp.where(is_main, 2 * (count - 1), 0))
    hop_load.wait()
    sigma_load.wait()
    eye = eye_mask(half)
    place = slab - in_far * cut

    def host_of(e):
        return host_row + e_local * mom + e

    def base_copy(e):
        return send(outgoing.at[e], base.at[place], s_base.at[e], r_base.at[place], slab=host_of(e))

    def coup_copy(e):
        return send(couple, coup.at[place], s_coup.at[e], r_coup.at[place], slab=host_of(e))

    def is_remote(e):
        return host_of(e) != slab

    def sends_coup(e):
        return jnp.logical_and(is_remote(e), jnp.logical_not(at_start))

    own_coup = pltpu.make_async_copy(couple, coup.at[place], s_in.at[0])

    @pl.when(is_main)
    def _():
        own_coup.start()

    for e in range(e_local):
        level = -0.5 + ((plane * e_local + e).astype(jnp.float32) + 0.5) / (depth * e_local) - onsite[...]
        real = on_diagonal(
            -hop[0] - sigma[e, 0],
            lambda block, n: block + jnp.where(eye, level[:, n * half : (n + 1) * half], 0.0),
        )
        imag = on_diagonal(
            -hop[1] - sigma[e, 1], lambda block, n: block + jnp.where(eye, ETA, 0.0)
        )

        @pl.when(is_remote(e))
        def _():
            store(outgoing.at[e], (real, imag))
            base_copy(e).start()

        @pl.when(jnp.logical_not(is_remote(e)))
        def _():
            store(base.at[place], (real, imag))

    for e in range(e_local):

        @pl.when(sends_coup(e))
        def _():
            coup_copy(e).start()

    def fill(e, carry):
        def entry(f, inner):
            value = jnp.float32(0.0)
            for mode in range(shifts.shape[0]):
                value = value + jnp.where(f == e + shifts[mode], weights[0, mode], 0.0)
                value = value + jnp.where(f == e - shifts[mode], weights[1, mode], 0.0)
            mix[e, f] = value * 0.5
            return inner

        return lax.fori_loop(0, depth * e_local, entry, carry)

    lax.fori_loop(0, depth * e_local, fill, 0)

    @pl.when(is_main)
    def _():
        own_coup.wait()

    def hcoup_copy(j):
        return send(coup.at[j], h_coup.at[j], s_hcoup.at[j], r_hcoup.at[j], mom=other)

    def hgreen_copy(j):
        return send(green.at[j + 1], h_green.at[j], s_hgreen.at[j], r_hgreen.at[j], mom=other)

    def hop_copy():
        return send(green.at[cut], green.at[0], s_hop.at[0], r_hop.at[0], slab=slab + far)

    def chain_copy(j):
        return send(h_chain.at[j + 1], chain.at[j], s_chain.at[j], r_chain.at[j], mom=other)

    def back_copy():
        return send(h_chain.at[0], h_chain.at[cut], s_back.at[0], r_back.at[0], slab=slab - far)

    def piece(n):
        return pl.ds(pl.multiple_of(lax.rem(plane * PIECES // depth + 1 + n, PIECES) * span, 8), span)

    def first_copy(j, part, n):
        return send(
            full.at[j, part, piece(n)], gathered.at[x, piece(n)], s_first.at[j, part, n],
            r_first.at[x, n], slab=offset + j, mom=part,
        )

    def is_first(j):
        return jnp.logical_and(is_near, j == 0)

    def is_last(j):
        return jnp.logical_and(is_far, j == count - 1)

    def first_remote(j, part):
        return jnp.logical_or(offset + j != slab, part != mom)

    @pl.when(is_main)
    def _():
        @pl.when(is_far)
        def _():
            arrived(green.at[0], r_hop.at[0])

        def forward(j, carry):
            @pl.when(j != place)
            def _():
                arrived(base.at[j], r_base.at[j])

            @pl.when(is_first(j))
            def _():
                left[...] = jnp.zeros_like(left)

            @pl.when(jnp.logical_not(is_first(j)))
            def _():
                @pl.when(j != place)
                def _():
                    arrived(coup.at[j], r_coup.at[j])

                hcoup_copy(j).start()
                coupling = load(coup.at[j])
                half_way = mul(prep(load(green.at[j])), prep_adjoint(coupling))
                store(left, mul(prep(coupling), prep(half_way)))

            store(
                green.at[j + 1],
                newton_inverse((base[j, 0] - left[0], base[j, 1] - left[1])),
            )

            @pl.when(jnp.logical_not(is_first(j)))
            def _():
                hgreen_copy(j).start()

            return carry

        lax.fori_loop(0, count, forward, 0)

        @pl.when(is_near)
        def _():
            hop_copy().start()

        def backward(turn, carry):
            j = count - 1 - turn

            @pl.when(is_last(j))
            def _():
                full[j] = green[j + 1]

            @pl.when(jnp.logical_not(is_last(j)))
            def _():
                arrived(chain.at[j], r_chain.at[j])
                pair = load(green.at[j + 1])
                ready = prep(pair)
                extra = mul(prep(mul(ready, prep(load(chain.at[j])))), ready)
                store(full.at[j], (pair[0] + extra[0], pair[1] + extra[1]))

            for n in range(PIECES):
                for part in range(2):

                    @pl.when(first_remote(j, part))
                    def _():
                        first_copy(j, part, n).start()

            for part in range(2):

                @pl.when(jnp.logical_not(first_remote(j, part)))
                def _():
                    gathered[x] = full[j, part]

            return carry

        lax.fori_loop(0, count, backward, 0)

    @pl.when(is_helper)
    def _():
        def forward(j, carry):
            @pl.when(jnp.logical_not(is_first(j)))
            def _():
                arrived(h_coup.at[j], r_hcoup.at[j])
                coupling = load(h_coup.at[j])
                adjoint = (coupling[0].T, -coupling[1].T)
                ready_left, ready_right = prep(adjoint), prep(coupling)
                store(h_adj.at[j], adjoint)
                arrived(h_green.at[j], r_hgreen.at[j])
                ready = prep(load(h_green.at[j]))
                store(h_first.at[j], mul(ready_left, ready))
                store(h_second.at[j], mul(ready, ready_right))

            return carry

        lax.fori_loop(0, count, forward, 0)

        @pl.when(is_far)
        def _():
            h_chain[slabs - cut] = jnp.zeros_like(h_chain.at[slabs - cut])

        @pl.when(is_near)
        def _():
            arrived(h_chain.at[cut], r_back.at[0])

        def backward(turn, carry):
            j = count - 1 - turn

            @pl.when(jnp.logical_not(is_last(j)))
            def _():
                chain_copy(j).start()

            @pl.when(jnp.logical_not(is_first(j)))
            def _():
                extra = mul(prep(load(h_first.at[j])), prep(load(h_chain.at[j + 1])))
                adjoint = load(h_adj.at[j])
                sums = (adjoint[0] + extra[0], adjoint[1] + extra[1])
                store(h_chain.at[j], mul(prep(sums), prep(load(h_second.at[j]))))

            return carry

        lax.fori_loop(0, count, backward, 0)

        @pl.when(is_far)
        def _():
            back_copy().start()

    def second_copy(target):
        return send(
            summed.at[:, pl.ds(pl.multiple_of(target * share, 8), share)], mixed.at[plane],
            s_second.at[target], r_second.at[plane], energy=target,
        )

    local_first = jnp.logical_and(is_main, hosted_here())
    per = depth // PIECES
    for n in range(PIECES):
        for c in range(ROW):

            @pl.when(jnp.logical_or(c != x, jnp.logical_not(local_first)))
            def _():
                arrived(gathered.at[c, piece(n)], r_first.at[c, n])

        for e in range(e_local):
            summed[e, piece(n)] = gathered[e, piece(n)] + gathered[e_local + e, piece(n)]
        for k in range(per):
            target = lax.rem(plane * PIECES // depth + 1 + n, PIECES) * per + k

            @pl.when(target != plane)
            def _():
                second_copy(target).start()

    def mixing(source, start):
        values = [mixed[source, e] for e in range(e_local)]

        def row(e, carry):
            value = mix[e, source * e_local] * values[0]
            for k in range(1, e_local):
                value = value + mix[e, source * e_local + k] * values[k]
            if start:
                total[e] = value
            else:
                total[e] = total[e] + value
            return carry

        lax.fori_loop(0, depth * e_local, row, 0)

    mixed[plane] = summed[:, pl.ds(pl.multiple_of(plane * share, 8), share)]
    mixing(plane, True)
    reach = [turn for step in range(1, depth // 2 + 1) for turn in sorted({step, depth - step})]
    for turn in reach:
        source = lax.rem(plane + turn, depth)
        arrived(mixed.at[source], r_second.at[source])
        mixing(source, False)

    out[:, mom] = total[...]
    last_copy = send(total, out.at[:, mom], s_last.at[0], r_last.at[0], mom=other)
    last_copy.start()

    for e in range(e_local):

        @pl.when(is_remote(e))
        def _():
            base_copy(e).wait_send()

        @pl.when(sends_coup(e))
        def _():
            coup_copy(e).wait_send()

    @pl.when(is_main)
    def _():
        def drain(j, carry):
            @pl.when(jnp.logical_not(is_first(j)))
            def _():
                hcoup_copy(j).wait_send()
                hgreen_copy(j).wait_send()

            for part in range(2):

                @pl.when(first_remote(j, part))
                def _():
                    for n in range(PIECES):
                        first_copy(j, part, n).wait_send()

            return carry

        lax.fori_loop(0, count, drain, 0)

        @pl.when(is_near)
        def _():
            hop_copy().wait_send()

    @pl.when(is_helper)
    def _():
        def drain(j, carry):
            @pl.when(jnp.logical_not(is_last(j)))
            def _():
                chain_copy(j).wait_send()

            return carry

        lax.fori_loop(0, count, drain, 0)

        @pl.when(is_far)
        def _():
            back_copy().wait_send()

    for turn in range(1, depth):
        second_copy(lax.rem(plane + turn, depth)).wait_send()
    last_copy.wait_send()
    arrived(out.at[:, other], r_last.at[0])


def body(onsite, hop, couple, sigma_in, shifts, mode_weight):
    e_local = sigma_in.shape[0]
    width = onsite.shape[-1]
    slabs = lax.axis_size("slab")
    depth = lax.axis_size("energy")
    total = e_local * depth
    share = width // depth
    block = (2, width, width)
    slots = max(CUT, slabs - CUT)

    def buffer(*shape):
        return pltpu.VMEM(shape, jnp.float32)

    def sems(*shape):
        return pltpu.SemaphoreType.DMA(shape)

    vmem = pl.BlockSpec(memory_space=pltpu.VMEM)
    smem = pl.BlockSpec(memory_space=pltpu.SMEM)
    stay = pl.BlockSpec(memory_space=pl.ANY)
    result = pl.pallas_call(
        functools.partial(kernel, CUT, slabs, depth, e_local),
        out_shape=jax.ShapeDtypeStruct((total, 2, share, width), jnp.float32),
        in_specs=[smem, smem, vmem, stay, stay, stay],
        out_specs=vmem,
        scratch_shapes=[
            buffer(*block),
            buffer(e_local, *block),
            buffer(e_local, *block),
            buffer(*block),
            buffer(slots, *block),
            buffer(slots, *block),
            buffer(slots + 1, *block),
            buffer(slots, *block),
            buffer(slots, *block),
            buffer(ROW, width, width),
            buffer(e_local, width, width),
            buffer(depth, e_local, share, width),
            buffer(total, share, width),
            pltpu.SMEM((total, total), jnp.float32),
            sems(2),
            sems(e_local), sems(slots), sems(e_local), sems(slots),
            sems(slots), sems(slots), sems(slots), sems(slots),
            sems(1), sems(1), sems(slots), sems(slots), sems(1), sems(1),
            sems(slots, 2, PIECES), sems(ROW, PIECES), sems(depth), sems(depth), sems(1), sems(1),
        ],
        compiler_params=pltpu.CompilerParams(
            collective_id=0, has_side_effects=True, vmem_limit_bytes=50 << 20
        ),
    )(shifts, mode_weight, onsite[0], hop[0, 0], couple[0, 0], sigma_in[:, 0])
    return result[:, None]


def solution(mesh):
    in_specs = (
        P("mom", "slab", None),
        P("mom", "slab", None, None, None),
        P("mom", "slab", None, None, None),
        P("energy", "slab", None, None, None),
        P(),
        P(),
    )
    out_specs = P(None, "slab", None, "energy", None)
    return jax.shard_map(body, mesh=mesh, in_specs=in_specs, out_specs=out_specs, check_vma=False)
```

time: 164 us -> 155 us (0.945)
  Pallas kernels: 159 us -> 150 us
    pallas_call x1, Pallas kernels: 159 us -> 150 us  [body(): pl.pallas_call(functools.partial(kernel, CUT, slabs, depth, e_local), out...]
    unnamed x7 -> x13, local copies, waits for them, and re-layouts: 3.67 us -> 4.97 us
where the time goes in v3:
time: 155 us
  Pallas kernels  150 us (97%)
  local copies, waits for them, and re-layouts  4.97 us (3%)
    pallas_call x1, Pallas kernels, body(): pl.pallas_call(functools.partial(kernel, CUT, slabs, depth, e_local), out...  150 us
    unnamed x13, local copies, waits for them, and re-layouts  4.97 us

profile of v3, /device:TPU:1, one launch (start us, length us, event | category | flops | bytes accessed | tf_op | source)
XLA Modules:
  0.0 154.8 jit_solution(18414054400187955232)
XLA Ops:
  0.0 0.0 copy-start.4
  0.0 0.0 copy-start.3
  0.0 0.0 copy-start.5
  0.0 0.7 copy-done.4
  0.7 0.0 copy-done.3
  0.7 0.0 copy-done.5
  0.7 0.0 copy-start
  0.7 1.2 copy-done
  1.9 0.0 copy-start.1
  1.9 1.0 copy-done.1
  3.0 0.0 copy-start.2
  3.0 1.0 copy-done.2
  4.0 149.9 %shard_map.64 = f32[16,2,32,256]{3,2,1,0:T(8,128)S(1)} custom-call(s32[4]{0:T(128)S(1)} %copy-done.5, f32[2,4]{1,0:T(2,128)S(1)} %copy-done.3, f32[1,256]{1,0:T(1,128)S(1)} %bitcast.11, f32[2,256,256]{2,1,0:T(8,128)S(1)} %bitcast.9, f32[2,256,256]{2,1,0:T(8,128)S(1)} %bitcast.10, f32[2,2,256,256]{3,2,1,0:T(8,128)S(1)} %bitcast.8), custom_call_target="tpu_custom_call" | custom-call | tf_op jit(solution)/shard_map/pallas_call | solution.py:524
  153.9 1.0 copy.9
Async XLA Ops:
  0.0 0.7 copy-start.4
  0.0 0.7 copy-start.3
  0.0 0.7 copy-start.5
  0.7 1.2 copy-start
  1.9 1.0 copy-start.1
  3.0 1.0 copy-start.2

commit v4 on v3

--- a/solution.py
+++ b/solution.py
@@ -10,6 +10,7 @@
 ETA = 0.5
 ROW = 4
 CUT = 6
+BACK = 4
 PIECES = 4
 MESH = pl.DeviceIdType.MESH
 
@@ -91,13 +92,13 @@
 
 
 def kernel(
-    cut, slabs, depth, e_local,
+    cut, turn_at, slabs, depth, e_local,
     shifts, weights, onsite, hop_in, couple, sigma_in, out,
     hop, sigma, outgoing, left, box_a, box_b, box_c, box_d, box_e, gathered, summed, mixed, total,
     mix, s_in,
     s_base, r_base, s_coup, r_coup, s_hcoup, r_hcoup, s_hgreen, r_hgreen,
     s_hop, r_hop, s_chain, r_chain, s_back, r_back, s_first, r_first,
-    s_second, r_second, s_last, r_last,
+    s_second, r_second, s_last, r_last, s_adopt, r_adopt, token,
 ):
     base = h_coup = h_adj = box_a
     coup = h_green = h_first = box_b
@@ -116,13 +117,16 @@
     near, far = 0, 2 * ROW
     in_far = jnp.where(slab >= cut, 1, 0)
     host_row = jnp.where(slab >= cut, far, near)
+    adopt = cut - turn_at
+    wide = slabs - turn_at
     is_near, is_far = y == 0, y == 2
     is_host = jnp.logical_or(is_near, is_far)
     is_main = jnp.logical_and(is_host, x // e_local == mom)
     is_helper = jnp.logical_and(is_host, x // e_local != mom)
     at_start = slab == 0
-    offset = jnp.where(is_near, 0, cut)
-    count = jnp.where(is_near, cut, slabs - cut)
+    offset = jnp.where(is_near, 0, turn_at)
+    count = jnp.where(is_near, turn_at, wide)
+    reach = jnp.where(is_near, cut, wide)
 
     def send(src, dst, send_sem, recv_sem, **where):
         return pltpu.make_async_remote_copy(
@@ -142,17 +146,18 @@
     def greet(**where):
         pl.semaphore_signal(barrier, inc=1, device_id=where, device_id_type=MESH)
 
-    def hosted_here():
-        return jnp.logical_and(is_host, y * ROW == host_row)
-
     greet(mom=other)
     for turn in range(1, depth):
         greet(energy=lax.rem(plane + turn, depth))
     for c in range(ROW):
 
-        @pl.when(host_row + c != slab)
-        def _():
-            greet(slab=host_row + c, mom=c // e_local)
+        @pl.when(jnp.logical_and(slab < cut, near + c != slab))
+        def _():
+            greet(slab=near + c, mom=c // e_local)
+
+        @pl.when(jnp.logical_and(slab >= turn_at, far + c != slab))
+        def _():
+            greet(slab=far + c, mom=c // e_local)
 
     @pl.when(is_host)
     def _():
@@ -168,14 +173,14 @@
 
             return carry
 
-        lax.fori_loop(0, count, call, 0)
-
-    expected = depth + ROW - jnp.where(hosted_here(), 1, 0) + jnp.where(is_host, 1, 0)
-    pl.semaphore_wait(barrier, expected + jnp.where(is_main, 2 * (count - 1), 0))
+        lax.fori_loop(0, reach, call, 0)
+
+    expected = depth + ROW * (jnp.where(slab < cut, 1, 0) + jnp.where(slab >= turn_at, 1, 0))
+    pl.semaphore_wait(barrier, expected + jnp.where(is_main, 2 * (reach - 1), 0))
     hop_load.wait()
     sigma_load.wait()
     eye = eye_mask(half)
-    place = slab - in_far * cut
+    place = slab - in_far * turn_at
 
     def host_of(e):
         return host_row + e_local * mom + e
@@ -247,13 +252,31 @@
         return send(green.at[j + 1], h_green.at[j], s_hgreen.at[j], r_hgreen.at[j], mom=other)
 
     def hop_copy():
-        return send(green.at[cut], green.at[0], s_hop.at[0], r_hop.at[0], slab=slab + far)
+        return send(green.at[cut], green.at[adopt], s_hop.at[0], r_hop.at[0], slab=slab + far)
+
+    def adopt_coup(a):
+        return send(coup.at[turn_at + a], coup.at[a], s_adopt.at[a], r_coup.at[a], slab=slab + far)
+
+    def adopt_green(a):
+        return send(
+            green.at[turn_at + a + 1], green.at[a + 1], s_adopt.at[adopt + a], r_adopt.at[a],
+            slab=slab + far,
+        )
+
+    def used(j):
+        return jnp.logical_and(
+            jnp.logical_not(is_first(j)), jnp.logical_or(is_far, j < turn_at)
+        )
+
+    def held(j, part):
+        late = offset + j >= slabs - ROW
+        return jnp.logical_and(late, part == 1)
 
     def chain_copy(j):
         return send(h_chain.at[j + 1], chain.at[j], s_chain.at[j], r_chain.at[j], mom=other)
 
     def back_copy():
-        return send(h_chain.at[0], h_chain.at[cut], s_back.at[0], r_back.at[0], slab=slab - far)
+        return send(h_chain.at[0], h_chain.at[turn_at], s_back.at[0], r_back.at[0], slab=slab - far)
 
     def piece(n):
         return pl.ds(pl.multiple_of(lax.rem(plane * PIECES // depth + 1 + n, PIECES) * span, 8), span)
@@ -277,7 +300,7 @@
     def _():
         @pl.when(is_far)
         def _():
-            arrived(green.at[0], r_hop.at[0])
+            arrived(green.at[adopt], r_hop.at[0])
 
         def forward(j, carry):
             @pl.when(j != place)
@@ -294,7 +317,10 @@
                 def _():
                     arrived(coup.at[j], r_coup.at[j])
 
-                hcoup_copy(j).start()
+                @pl.when(used(j))
+                def _():
+                    hcoup_copy(j).start()
+
                 coupling = load(coup.at[j])
                 half_way = mul(prep(load(green.at[j])), prep_adjoint(coupling))
                 store(left, mul(prep(coupling), prep(half_way)))
@@ -304,17 +330,31 @@
                 newton_inverse((base[j, 0] - left[0], base[j, 1] - left[1])),
             )
 
-            @pl.when(jnp.logical_not(is_first(j)))
+            @pl.when(used(j))
             def _():
                 hgreen_copy(j).start()
 
-            return carry
-
-        lax.fori_loop(0, count, forward, 0)
+            @pl.when(jnp.logical_and(is_far, j == wide - 3))
+            def _():
+                for a in range(adopt):
+                    arrived(coup.at[a], r_coup.at[a])
+                    if a < adopt - 1:
+                        arrived(green.at[a + 1], r_adopt.at[a])
+                    hcoup_copy(a).start()
+                    hgreen_copy(a).start()
+
+            return carry
+
+        lax.fori_loop(jnp.where(is_near, 0, adopt), reach, forward, 0)
 
         @pl.when(is_near)
         def _():
             hop_copy().start()
+            hop_copy().wait_send()
+            for a in range(adopt):
+                adopt_coup(a).start()
+                if a < adopt - 1:
+                    adopt_green(a).start()
 
         def backward(turn, carry):
             j = count - 1 - turn
@@ -333,8 +373,11 @@
 
             for n in range(PIECES):
                 for part in range(2):
-
-                    @pl.when(first_remote(j, part))
+                    now = jnp.logical_and(is_far, jnp.logical_not(held(j, part)))
+                    if n == 0:
+                        now = jnp.logical_or(is_near, now)
+
+                    @pl.when(jnp.logical_and(first_remote(j, part), now))
                     def _():
                         first_copy(j, part, n).start()
 
@@ -348,9 +391,48 @@
 
         lax.fori_loop(0, count, backward, 0)
 
+        @pl.when(is_near)
+        def _():
+            def sweep(n, act):
+                def one(j, carry):
+                    for part in range(2):
+
+                        @pl.when(first_remote(j, part))
+                        def _():
+                            act(first_copy(j, part, n))
+
+                    return carry
+
+                lax.fori_loop(0, count, one, 0)
+
+            for n in range(1, PIECES):
+                sweep(n, lambda copy: copy.start())
+                sweep(n - 1, lambda copy: copy.wait_send())
+            sweep(PIECES - 1, lambda copy: copy.wait_send())
+
+        @pl.when(is_far)
+        def _():
+            pl.semaphore_wait(token, 1)
+
+            def release(j, carry):
+                for part in range(2):
+
+                    @pl.when(jnp.logical_and(first_remote(j, part), held(j, part)))
+                    def _():
+                        for n in range(PIECES):
+                            first_copy(j, part, n).start()
+
+                return carry
+
+            lax.fori_loop(0, count, release, 0)
+
     @pl.when(is_helper)
     def _():
-        def forward(j, carry):
+        def forward(step, carry):
+            early = wide - 2 - adopt
+            late = jnp.where(step < early + adopt, step - early, step)
+            j = jnp.where(is_near, step, jnp.where(step < early, step + adopt, late))
+
             @pl.when(jnp.logical_not(is_first(j)))
             def _():
                 arrived(h_coup.at[j], r_hcoup.at[j])
@@ -369,11 +451,11 @@
 
         @pl.when(is_far)
         def _():
-            h_chain[slabs - cut] = jnp.zeros_like(h_chain.at[slabs - cut])
+            h_chain[wide] = jnp.zeros_like(h_chain.at[wide])
 
         @pl.when(is_near)
         def _():
-            arrived(h_chain.at[cut], r_back.at[0])
+            arrived(h_chain.at[turn_at], r_back.at[0])
 
         def backward(turn, carry):
             j = count - 1 - turn
@@ -396,6 +478,8 @@
         @pl.when(is_far)
         def _():
             back_copy().start()
+            back_copy().wait_send()
+            pl.semaphore_signal(token, inc=1, device_id={"mom": other}, device_id_type=MESH)
 
     def second_copy(target):
         return send(
@@ -403,7 +487,7 @@
             s_second.at[target], r_second.at[plane], energy=target,
         )
 
-    local_first = jnp.logical_and(is_main, hosted_here())
+    local_first = is_main
     per = depth // PIECES
     for n in range(PIECES):
         for c in range(ROW):
@@ -438,8 +522,8 @@
 
     mixed[plane] = summed[:, pl.ds(pl.multiple_of(plane * share, 8), share)]
     mixing(plane, True)
-    reach = [turn for step in range(1, depth // 2 + 1) for turn in sorted({step, depth - step})]
-    for turn in reach:
+    order = [turn for step in range(1, depth // 2 + 1) for turn in sorted({step, depth - step})]
+    for turn in order:
         source = lax.rem(plane + turn, depth)
         arrived(mixed.at[source], r_second.at[source])
         mixing(source, False)
@@ -461,14 +545,14 @@
     @pl.when(is_main)
     def _():
         def drain(j, carry):
-            @pl.when(jnp.logical_not(is_first(j)))
+            @pl.when(used(j))
             def _():
                 hcoup_copy(j).wait_send()
                 hgreen_copy(j).wait_send()
 
             for part in range(2):
 
-                @pl.when(first_remote(j, part))
+                @pl.when(jnp.logical_and(is_far, first_remote(j, part)))
                 def _():
                     for n in range(PIECES):
                         first_copy(j, part, n).wait_send()
@@ -479,7 +563,10 @@
 
         @pl.when(is_near)
         def _():
-            hop_copy().wait_send()
+            for a in range(adopt):
+                adopt_coup(a).wait_send()
+                if a < adopt - 1:
+                    adopt_green(a).wait_send()
 
     @pl.when(is_helper)
     def _():
@@ -491,10 +578,6 @@
             return carry
 
         lax.fori_loop(0, count, drain, 0)
-
-        @pl.when(is_far)
-        def _():
-            back_copy().wait_send()
 
     for turn in range(1, depth):
         second_copy(lax.rem(plane + turn, depth)).wait_send()
@@ -510,7 +593,7 @@
     total = e_local * depth
     share = width // depth
     block = (2, width, width)
-    slots = max(CUT, slabs - CUT)
+    slots = max(CUT, slabs - BACK)
 
     def buffer(*shape):
         return pltpu.VMEM(shape, jnp.float32)
@@ -520,9 +603,9 @@
 
     vmem = pl.BlockSpec(memory_space=pltpu.VMEM)
     smem = pl.BlockSpec(memory_space=pltpu.SMEM)
-    stay = pl.BlockSpec(memory_space=pl.ANY)
+    stay = pl.BlockSpec(memory_space=pltpu.HBM)
     result = pl.pallas_call(
-        functools.partial(kernel, CUT, slabs, depth, e_local),
+        functools.partial(kernel, CUT, BACK, slabs, depth, e_local),
         out_shape=jax.ShapeDtypeStruct((total, 2, share, width), jnp.float32),
         in_specs=[smem, smem, vmem, stay, stay, stay],
         out_specs=vmem,
@@ -546,6 +629,7 @@
             sems(slots), sems(slots), sems(slots), sems(slots),
             sems(1), sems(1), sems(slots), sems(slots), sems(1), sems(1),
             sems(slots, 2, PIECES), sems(ROW, PIECES), sems(depth), sems(depth), sems(1), sems(1),
+            sems(2 * (CUT - BACK)), sems(CUT - BACK), pltpu.SemaphoreType.REGULAR,
         ],
         compiler_params=pltpu.CompilerParams(
             collective_id=0, has_side_effects=True, vmem_limit_bytes=50 << 20

time: 155 us -> 143 us (0.923)
  the two profiles are of different devices: /device:TPU:1 before, /device:TPU:11 now
where the time goes in v4:
time: 143 us
  Pallas kernels  138 us (97%)
  local copies, waits for them, and re-layouts  4.97 us (3%)
    pallas_call x1, Pallas kernels, body(): pl.pallas_call(functools.partial(kernel, CUT, BACK, slabs, depth, e_local...  138 us
    unnamed x13, local copies, waits for them, and re-layouts  4.97 us

profile of v4, /device:TPU:11, one launch (start us, length us, event | category | flops | bytes accessed | tf_op | source)
XLA Modules:
  0.0 142.8 jit_solution(14735500803580271113)
XLA Ops:
  0.0 0.0 copy-start.4
  0.0 0.0 copy-start.3
  0.0 0.0 copy-start.5
  0.0 0.7 copy-done.4
  0.7 0.0 copy-done.3
  0.7 0.0 copy-done.5
  0.7 0.0 copy-start
  0.7 1.2 copy-done
  1.9 0.0 copy-start.1
  1.9 1.0 copy-done.1
  3.0 0.0 copy-start.2
  3.0 1.0 copy-done.2
  4.0 137.8 %shard_map.64 = f32[16,2,32,256]{3,2,1,0:T(8,128)S(1)} custom-call(s32[4]{0:T(128)S(1)} %copy-done.5, f32[2,4]{1,0:T(2,128)S(1)} %copy-done.3, f32[1,256]{1,0:T(1,128)S(1)} %bitcast.11, f32[2,256,256]{2,1,0:T(8,128)S(1)} %bitcast.9, f32[2,256,256]{2,1,0:T(8,128)S(1)} %bitcast.10, f32[2,2,256,256]{3,2,1,0:T(8,128)S(1)} %bitcast.8), custom_call_target="tpu_custom_call" | custom-call | tf_op jit(solution)/shard_map/pallas_call | solution.py:607
  141.8 1.0 copy.9
Async XLA Ops:
  0.0 0.7 copy-start.4
  0.0 0.7 copy-start.3
  0.0 0.7 copy-start.5
  0.7 1.2 copy-start
  1.9 1.0 copy-start.1
  3.0 1.0 copy-start.2

commit v5 on v4

--- a/solution.py
+++ b/solution.py
@@ -98,7 +98,7 @@
     mix, s_in,
     s_base, r_base, s_coup, r_coup, s_hcoup, r_hcoup, s_hgreen, r_hgreen,
     s_hop, r_hop, s_chain, r_chain, s_back, r_back, s_first, r_first,
-    s_second, r_second, s_last, r_last, s_adopt, r_adopt, token,
+    s_second, r_second, s_last, r_last, s_adopt, r_adopt, r_relay, token,
 ):
     base = h_coup = h_adj = box_a
     coup = h_green = h_first = box_b
@@ -163,6 +163,11 @@
     def _():
         greet(slab=far - y * ROW + x)
 
+    @pl.when(jnp.logical_not(is_host))
+    def _():
+        for turn in range(1, ROW):
+            greet(slab=y * ROW + lax.rem(x + turn, ROW))
+
     @pl.when(is_main)
     def _():
         def call(j, carry):
@@ -176,6 +181,7 @@
         lax.fori_loop(0, reach, call, 0)
 
     expected = depth + ROW * (jnp.where(slab < cut, 1, 0) + jnp.where(slab >= turn_at, 1, 0))
+    expected = expected + jnp.where(is_host, 0, ROW - 1)
     pl.semaphore_wait(barrier, expected + jnp.where(is_main, 2 * (reach - 1), 0))
     hop_load.wait()
     sigma_load.wait()
@@ -287,6 +293,25 @@
             r_first.at[x, n], slab=offset + j, mom=part,
         )
 
+    def relay_copy(j, part, side):
+        where = pl.ds(side * half, half)
+        return send(
+            full.at[j, part, where], full.at[lax.rem(offset + j, ROW), part, where],
+            s_first.at[j, part, side], r_relay.at[lax.rem(offset + j, ROW), side],
+            slab=(offset + j) // ROW * ROW + x, mom=part,
+        )
+
+    def relayed(j):
+        return jnp.logical_and(is_far, (offset + j) // ROW != 2)
+
+    def pass_copy(r, part):
+        where = pl.ds(part * span, span)
+        order = lax.rem(part + 2 * PIECES - 1 - plane * PIECES // depth, PIECES)
+        return send(
+            full.at[r, mom, where], gathered.at[x, where], s_first.at[r, 0, part],
+            r_first.at[x, order], slab=y * ROW + r,
+        )
+
     def is_first(j):
         return jnp.logical_and(is_near, j == 0)
 
@@ -373,7 +398,7 @@
 
             for n in range(PIECES):
                 for part in range(2):
-                    now = jnp.logical_and(is_far, jnp.logical_not(held(j, part)))
+                    now = jnp.logical_and(is_far, jnp.logical_not(relayed(j)))
                     if n == 0:
                         now = jnp.logical_or(is_near, now)
 
@@ -382,6 +407,11 @@
                         first_copy(j, part, n).start()
 
             for part in range(2):
+
+                @pl.when(jnp.logical_and(relayed(j), jnp.logical_not(held(j, part))))
+                def _():
+                    for side in range(2):
+                        relay_copy(j, part, side).start()
 
                 @pl.when(jnp.logical_not(first_remote(j, part)))
                 def _():
@@ -417,10 +447,10 @@
             def release(j, carry):
                 for part in range(2):
 
-                    @pl.when(jnp.logical_and(first_remote(j, part), held(j, part)))
+                    @pl.when(held(j, part))
                     def _():
-                        for n in range(PIECES):
-                            first_copy(j, part, n).start()
+                        for side in range(2):
+                            relay_copy(j, part, side).start()
 
                 return carry
 
@@ -487,7 +517,28 @@
             s_second.at[target], r_second.at[plane], energy=target,
         )
 
-    local_first = is_main
+    @pl.when(jnp.logical_not(is_host))
+    def _():
+        def hand_on(turn, carry):
+            r = ROW - 1 - turn
+            for side in range(2):
+                where = pl.ds(side * half, half)
+                arrived(full.at[r, mom, where], r_relay.at[r, side])
+
+                @pl.when(r != x)
+                def _():
+                    for part in range(side * PIECES // 2, (side + 1) * PIECES // 2):
+                        pass_copy(r, part).start()
+
+                @pl.when(r == x)
+                def _():
+                    gathered[x, where] = full[r, mom, where]
+
+            return carry
+
+        lax.fori_loop(0, ROW, hand_on, 0)
+
+    local_first = jnp.logical_or(is_main, jnp.logical_not(is_host))
     per = depth // PIECES
     for n in range(PIECES):
         for c in range(ROW):
@@ -508,17 +559,11 @@
     def mixing(source, start):
         values = [mixed[source, e] for e in range(e_local)]
 
-        def row(e, carry):
+        for e in range(depth * e_local):
             value = mix[e, source * e_local] * values[0]
             for k in range(1, e_local):
                 value = value + mix[e, source * e_local + k] * values[k]
-            if start:
-                total[e] = value
-            else:
-                total[e] = total[e] + value
-            return carry
-
-        lax.fori_loop(0, depth * e_local, row, 0)
+            total[e] = value if start else total[e] + value
 
     mixed[plane] = summed[:, pl.ds(pl.multiple_of(plane * share, 8), share)]
     mixing(plane, True)
@@ -552,10 +597,17 @@
 
             for part in range(2):
 
-                @pl.when(jnp.logical_and(is_far, first_remote(j, part)))
+                direct = jnp.logical_and(is_far, jnp.logical_not(relayed(j)))
+
+                @pl.when(jnp.logical_and(direct, first_remote(j, part)))
                 def _():
                     for n in range(PIECES):
                         first_copy(j, part, n).wait_send()
+
+                @pl.when(relayed(j))
+                def _():
+                    for side in range(2):
+                        relay_copy(j, part, side).wait_send()
 
             return carry
 
@@ -567,6 +619,15 @@
                 adopt_coup(a).wait_send()
                 if a < adopt - 1:
                     adopt_green(a).wait_send()
+
+    @pl.when(jnp.logical_not(is_host))
+    def _():
+        for r in range(ROW):
+
+            @pl.when(r != x)
+            def _():
+                for part in range(PIECES):
+                    pass_copy(r, part).wait_send()
 
     @pl.when(is_helper)
     def _():
@@ -629,10 +690,10 @@
             sems(slots), sems(slots), sems(slots), sems(slots),
             sems(1), sems(1), sems(slots), sems(slots), sems(1), sems(1),
             sems(slots, 2, PIECES), sems(ROW, PIECES), sems(depth), sems(depth), sems(1), sems(1),
-            sems(2 * (CUT - BACK)), sems(CUT - BACK), pltpu.SemaphoreType.REGULAR,
+            sems(2 * (CUT - BACK)), sems(CUT - BACK), sems(ROW, 2), pltpu.SemaphoreType.REGULAR,
         ],
         compiler_params=pltpu.CompilerParams(
-            collective_id=0, has_side_effects=True, vmem_limit_bytes=50 << 20
+            collective_id=0, has_side_effects=True, vmem_limit_bytes=56 << 20
         ),
     )(shifts, mode_weight, onsite[0], hop[0, 0], couple[0, 0], sigma_in[:, 0])
     return result[:, None]

time: 143 us -> 139 us (0.972)
  the two profiles are of different devices: /device:TPU:11 before, /device:TPU:9 now
where the time goes in v5:
time: 139 us; the launch traced here: 138 us
  Pallas kernels  136 us (98%)
  local copies, waits for them, and re-layouts  2.31 us (2%)
    pallas_call x1, Pallas kernels, body(): pl.pallas_call(functools.partial(kernel, CUT, BACK, slabs, depth, e_local...  136 us

profile of v5, /device:TPU:9, one launch (start us, length us, event | category | flops | bytes accessed | tf_op | source)
XLA Modules:
  0.0 138.4 jit_solution(15169638026724474763)
XLA Ops:
  0.0 136.1 %shard_map.64 = f32[16,2,32,256]{3,2,1,0:T(8,128)} custom-call(s32[4]{0:T(128)} %shifts.1, f32[2,4]{1,0:T(2,128)} %weights.1, f32[1,256]{1,0:T(1,128)} %bitcast.11, f32[2,256,256]{2,1,0:T(8,128)} %bitcast.9, f32[2,256,256]{2,1,0:T(8,128)} %bitcast.10, f32[2,2,256,256]{3,2,1,0:T(8,128)} %bitcast.8), custom_call_target="tpu_custom_call" | custom-call | tf_op jit(solution)/shard_map/pallas_call | solution.py:668
  136.1 2.3 %copy.9 = f32[16,1,2,32,256]{4,3,2,1,0:T(8,128)} copy(f32[16,1,2,32,256]{4,3,2,1,0:T(8,128)} %bitcast.7) | data formatting | bytes 2097152

commit v6 on v5

--- a/solution.py
+++ b/solution.py
@@ -10,7 +10,7 @@
 ETA = 0.5
 ROW = 4
 CUT = 6
-BACK = 4
+BACK = 5
 PIECES = 4
 MESH = pl.DeviceIdType.MESH
 
@@ -98,7 +98,7 @@
     mix, s_in,
     s_base, r_base, s_coup, r_coup, s_hcoup, r_hcoup, s_hgreen, r_hgreen,
     s_hop, r_hop, s_chain, r_chain, s_back, r_back, s_first, r_first,
-    s_second, r_second, s_last, r_last, s_adopt, r_adopt, r_relay, token,
+    s_second, r_second, s_last, r_last, s_adopt, r_adopt, r_relay, s_detour, r_detour, token,
 ):
     base = h_coup = h_adj = box_a
     coup = h_green = h_first = box_b
@@ -146,16 +146,23 @@
     def greet(**where):
         pl.semaphore_signal(barrier, inc=1, device_id=where, device_id_type=MESH)
 
+    in_upper, in_lower = slab < 2 * ROW, slab >= ROW
+    opposite = lax.rem(x + 2, ROW)
+    is_detour = opposite // e_local == mom
+    is_relay = jnp.logical_and(y == 3, is_detour)
+    starts_detour = jnp.logical_and(y == 0, is_detour)
+    members = jnp.where(is_near, 2 * ROW, slabs - ROW)
+    first_member = jnp.where(is_near, 0, ROW)
     greet(mom=other)
     for turn in range(1, depth):
         greet(energy=lax.rem(plane + turn, depth))
     for c in range(ROW):
 
-        @pl.when(jnp.logical_and(slab < cut, near + c != slab))
+        @pl.when(jnp.logical_and(in_upper, near + c != slab))
         def _():
             greet(slab=near + c, mom=c // e_local)
 
-        @pl.when(jnp.logical_and(slab >= turn_at, far + c != slab))
+        @pl.when(jnp.logical_and(in_lower, far + c != slab))
         def _():
             greet(slab=far + c, mom=c // e_local)
 
@@ -171,18 +178,33 @@
     @pl.when(is_main)
     def _():
         def call(j, carry):
-            @pl.when(offset + j != slab)
-            def _():
-                greet(slab=offset + j, mom=mom)
-                greet(slab=offset + j, mom=other)
+            @pl.when(first_member + j != slab)
+            def _():
+                greet(slab=first_member + j, mom=mom)
+                greet(slab=first_member + j, mom=other)
 
             return carry
 
-        lax.fori_loop(0, reach, call, 0)
-
-    expected = depth + ROW * (jnp.where(slab < cut, 1, 0) + jnp.where(slab >= turn_at, 1, 0))
+        lax.fori_loop(0, members, call, 0)
+
+        @pl.when(is_near)
+        def _():
+            greet(slab=3 * ROW + opposite)
+
+    @pl.when(starts_detour)
+    def _():
+        greet(slab=3 * ROW + x)
+
+    @pl.when(is_relay)
+    def _():
+        greet(slab=x)
+        greet(slab=opposite)
+
+    expected = depth + ROW * (jnp.where(in_upper, 1, 0) + jnp.where(in_lower, 1, 0))
     expected = expected + jnp.where(is_host, 0, ROW - 1)
-    pl.semaphore_wait(barrier, expected + jnp.where(is_main, 2 * (reach - 1), 0))
+    expected = expected + jnp.where(jnp.logical_and(is_main, is_near), 1, 0)
+    expected = expected + jnp.where(starts_detour, 1, 0) + jnp.where(is_relay, 2, 0)
+    pl.semaphore_wait(barrier, expected + jnp.where(is_main, 2 * (members - 1), 0))
     hop_load.wait()
     sigma_load.wait()
     eye = eye_mask(half)
@@ -200,8 +222,27 @@
     def is_remote(e):
         return host_of(e) != slab
 
+    def detours(e):
+        return jnp.logical_and(y == 0, host_of(e) == opposite)
+
+    def straight(e):
+        return jnp.logical_and(is_remote(e), jnp.logical_not(detours(e)))
+
     def sends_coup(e):
-        return jnp.logical_and(is_remote(e), jnp.logical_not(at_start))
+        return jnp.logical_and(straight(e), jnp.logical_not(at_start))
+
+    def detour_copy(src, q):
+        return send(
+            src, box_a.at[q // 2, q % 2], s_detour.at[q], r_detour.at[q], slab=slab + 3 * ROW
+        )
+
+    def pass_in(q):
+        target, sem = (base, r_base) if q < 2 else (coup, r_coup)
+        return send(
+            box_a.at[q // 2, q % 2], target.at[x, q % 2], s_detour.at[q], sem.at[x], slab=opposite
+        )
+
+    has_coup = x != 0
 
     own_coup = pltpu.make_async_copy(couple, coup.at[place], s_in.at[0])
 
@@ -222,16 +263,43 @@
         @pl.when(is_remote(e))
         def _():
             store(outgoing.at[e], (real, imag))
+
+        @pl.when(jnp.logical_and(straight(e), jnp.logical_not(is_relay)))
+        def _():
             base_copy(e).start()
 
+        @pl.when(detours(e))
+        def _():
+            for part in range(2):
+                detour_copy(outgoing.at[e, part], part).start()
+
         @pl.when(jnp.logical_not(is_remote(e)))
         def _():
             store(base.at[place], (real, imag))
 
     for e in range(e_local):
 
-        @pl.when(sends_coup(e))
-        def _():
+        @pl.when(jnp.logical_and(sends_coup(e), jnp.logical_not(is_relay)))
+        def _():
+            coup_copy(e).start()
+
+        @pl.when(jnp.logical_and(detours(e), has_coup))
+        def _():
+            for part in range(2):
+                detour_copy(couple.at[part], 2 + part).start()
+
+    @pl.when(is_relay)
+    def _():
+        for q in range(4):
+
+            @pl.when(jnp.logical_or(q < 2, has_coup))
+            def _():
+                arrived(box_a.at[q // 2, q % 2], r_detour.at[q])
+                pass_in(q).start()
+
+        for e in range(e_local):
+            base_copy(e).start()
+        for e in range(e_local):
             coup_copy(e).start()
 
     def fill(e, carry):
@@ -240,7 +308,7 @@
             for mode in range(shifts.shape[0]):
                 value = value + jnp.where(f == e + shifts[mode], weights[0, mode], 0.0)
                 value = value + jnp.where(f == e - shifts[mode], weights[1, mode], 0.0)
-            mix[e, f] = value * 0.5
+            mix[e, f] = value
             return inner
 
         return lax.fori_loop(0, depth * e_local, entry, carry)
@@ -302,7 +370,7 @@
         )
 
     def relayed(j):
-        return jnp.logical_and(is_far, (offset + j) // ROW != 2)
+        return (offset + j) // ROW != y
 
     def pass_copy(r, part):
         where = pl.ds(part * span, span)
@@ -400,7 +468,7 @@
                 for part in range(2):
                     now = jnp.logical_and(is_far, jnp.logical_not(relayed(j)))
                     if n == 0:
-                        now = jnp.logical_or(is_near, now)
+                        now = jnp.logical_or(jnp.logical_and(is_near, jnp.logical_not(relayed(j))), now)
 
                     @pl.when(jnp.logical_and(first_remote(j, part), now))
                     def _():
@@ -427,7 +495,7 @@
                 def one(j, carry):
                     for part in range(2):
 
-                        @pl.when(first_remote(j, part))
+                        @pl.when(jnp.logical_and(first_remote(j, part), jnp.logical_not(relayed(j))))
                         def _():
                             act(first_copy(j, part, n))
 
@@ -579,9 +647,17 @@
 
     for e in range(e_local):
 
-        @pl.when(is_remote(e))
+        @pl.when(straight(e))
         def _():
             base_copy(e).wait_send()
+
+        @pl.when(detours(e))
+        def _():
+            for q in range(4):
+
+                @pl.when(jnp.logical_or(q < 2, has_coup))
+                def _():
+                    detour_copy(outgoing.at[e, q % 2], q).wait_send()
 
         @pl.when(sends_coup(e))
         def _():
@@ -619,6 +695,14 @@
                 adopt_coup(a).wait_send()
                 if a < adopt - 1:
                     adopt_green(a).wait_send()
+
+    @pl.when(is_relay)
+    def _():
+        for q in range(4):
+
+            @pl.when(jnp.logical_or(q < 2, has_coup))
+            def _():
+                pass_in(q).wait_send()
 
     @pl.when(jnp.logical_not(is_host))
     def _():
@@ -690,13 +774,13 @@
             sems(slots), sems(slots), sems(slots), sems(slots),
             sems(1), sems(1), sems(slots), sems(slots), sems(1), sems(1),
             sems(slots, 2, PIECES), sems(ROW, PIECES), sems(depth), sems(depth), sems(1), sems(1),
-            sems(2 * (CUT - BACK)), sems(CUT - BACK), sems(ROW, 2), pltpu.SemaphoreType.REGULAR,
+            sems(2 * (CUT - BACK)), sems(CUT - BACK), sems(ROW, 2), sems(4), sems(4), pltpu.SemaphoreType.REGULAR,
         ],
         compiler_params=pltpu.CompilerParams(
             collective_id=0, has_side_effects=True, vmem_limit_bytes=56 << 20
         ),
     )(shifts, mode_weight, onsite[0], hop[0, 0], couple[0, 0], sigma_in[:, 0])
-    return result[:, None]
+    return result[:, None] / lax.axis_size("mom")
 
 
 def solution(mesh):

time: 139 us -> 135 us (0.971)
  the two profiles are of different devices: /device:TPU:9 before, /device:TPU:1 now
where the time goes in v6:
time: 135 us
  Pallas kernels  132 us (98%)
  other arithmetic  2.31 us (2%)
    pallas_call x1, Pallas kernels, body(): pl.pallas_call(functools.partial(kernel, CUT, BACK, slabs, depth, e_local...  132 us

profile of v6, /device:TPU:1, one launch (start us, length us, event | category | flops | bytes accessed | tf_op | source)
XLA Modules:
  0.0 134.5 jit_solution(5855146764886403914)
XLA Ops:
  0.0 132.2 %shard_map.64 = f32[16,2,32,256]{3,2,1,0:T(8,128)} custom-call(s32[4]{0:T(128)} %shifts.1, f32[2,4]{1,0:T(2,128)} %weights.1, f32[1,256]{1,0:T(1,128)} %bitcast.11, f32[2,256,256]{2,1,0:T(8,128)} %bitcast.9, f32[2,256,256]{2,1,0:T(8,128)} %bitcast.10, f32[2,2,256,256]{3,2,1,0:T(8,128)} %bitcast.8), custom_call_target="tpu_custom_call" | custom-call | tf_op jit(solution)/shard_map/pallas_call | solution.py:752
  132.2 2.3 %multiply_bitcast_fusion = f32[16,1,2,32,256]{4,3,2,1,0:T(8,128)} fusion(f32[16,2,32,256]{3,2,1,0:T(8,128)} %shard_map.64), kind=kLoop, calls=%fused_computation | loop fusion | flops 262144 | bytes 2097152 | tf_op jit(solution)/shard_map/div | solution.py:783

commit v7 on v5

--- a/solution.py
+++ b/solution.py
@@ -10,8 +10,9 @@
 ETA = 0.5
 ROW = 4
 CUT = 6
-BACK = 4
+BACK = 5
 PIECES = 4
+FINAL = 8
 MESH = pl.DeviceIdType.MESH
 
 
@@ -98,7 +99,7 @@
     mix, s_in,
     s_base, r_base, s_coup, r_coup, s_hcoup, r_hcoup, s_hgreen, r_hgreen,
     s_hop, r_hop, s_chain, r_chain, s_back, r_back, s_first, r_first,
-    s_second, r_second, s_last, r_last, s_adopt, r_adopt, r_relay, token,
+    s_second, r_second, s_last, r_last, s_adopt, r_adopt, r_relay, s_detour, r_detour, token,
 ):
     base = h_coup = h_adj = box_a
     coup = h_green = h_first = box_b
@@ -146,43 +147,60 @@
     def greet(**where):
         pl.semaphore_signal(barrier, inc=1, device_id=where, device_id_type=MESH)
 
+    opposite = lax.rem(x + 2, ROW)
+    is_detour = opposite // e_local == mom
+    is_relay = jnp.logical_and(y == 3, is_detour)
+    starts_detour = jnp.logical_and(y == 0, jnp.logical_and(is_detour, x != 0))
+    passes = jnp.logical_and(is_relay, x != 0)
     greet(mom=other)
     for turn in range(1, depth):
         greet(energy=lax.rem(plane + turn, depth))
+
+    @pl.when(is_main)
+    def _():
+        first_source = jnp.where(is_near, 0, cut)
+
+        def call(j, carry):
+            @pl.when(first_source + j != slab)
+            def _():
+                greet(slab=first_source + j)
+
+            return carry
+
+        lax.fori_loop(0, jnp.where(is_near, cut, slabs - cut), call, 0)
+
+        @pl.when(jnp.logical_and(is_near, x != 2))
+        def _():
+            greet(slab=3 * ROW + opposite)
+
+        @pl.when(is_far)
+        def _():
+            greet(slab=x)
+
+    @pl.when(jnp.logical_and(is_near, jnp.logical_not(is_main)))
+    def _():
+        greet(slab=far + x)
+
+    @pl.when(passes)
+    def _():
+        greet(slab=x)
+
     for c in range(ROW):
 
-        @pl.when(jnp.logical_and(slab < cut, near + c != slab))
-        def _():
-            greet(slab=near + c, mom=c // e_local)
-
-        @pl.when(jnp.logical_and(slab >= turn_at, far + c != slab))
-        def _():
-            greet(slab=far + c, mom=c // e_local)
-
-    @pl.when(is_host)
-    def _():
-        greet(slab=far - y * ROW + x)
+        @pl.when(jnp.logical_and(is_host, x != c))
+        def _():
+            greet(slab=y * ROW + c, mom=c // e_local)
 
     @pl.when(jnp.logical_not(is_host))
     def _():
+        greet(slab=far + x, mom=x // e_local)
         for turn in range(1, ROW):
             greet(slab=y * ROW + lax.rem(x + turn, ROW))
 
-    @pl.when(is_main)
-    def _():
-        def call(j, carry):
-            @pl.when(offset + j != slab)
-            def _():
-                greet(slab=offset + j, mom=mom)
-                greet(slab=offset + j, mom=other)
-
-            return carry
-
-        lax.fori_loop(0, reach, call, 0)
-
-    expected = depth + ROW * (jnp.where(slab < cut, 1, 0) + jnp.where(slab >= turn_at, 1, 0))
-    expected = expected + jnp.where(is_host, 0, ROW - 1)
-    pl.semaphore_wait(barrier, expected + jnp.where(is_main, 2 * (reach - 1), 0))
+    @pl.when(y == 1)
+    def _():
+        greet(slab=near + x, mom=x // e_local)
+
     hop_load.wait()
     sigma_load.wait()
     eye = eye_mask(half)
@@ -200,14 +218,25 @@
     def is_remote(e):
         return host_of(e) != slab
 
+    def detours(e):
+        return jnp.logical_and(y == 0, host_of(e) == opposite)
+
     def sends_coup(e):
-        return jnp.logical_and(is_remote(e), jnp.logical_not(at_start))
+        direct = jnp.logical_and(is_remote(e), jnp.logical_not(detours(e)))
+        return jnp.logical_and(direct, jnp.logical_not(at_start))
+
+    def detour_copy(part):
+        return send(
+            couple.at[part], box_a.at[0, part], s_detour.at[part], r_detour.at[part],
+            slab=slab + 3 * ROW,
+        )
+
+    def pass_in(part):
+        return send(
+            box_a.at[0, part], coup.at[x, part], s_detour.at[part], r_coup.at[x], slab=opposite
+        )
 
     own_coup = pltpu.make_async_copy(couple, coup.at[place], s_in.at[0])
-
-    @pl.when(is_main)
-    def _():
-        own_coup.start()
 
     for e in range(e_local):
         level = -0.5 + ((plane * e_local + e).astype(jnp.float32) + 0.5) / (depth * e_local) - onsite[...]
@@ -218,20 +247,48 @@
         imag = on_diagonal(
             -hop[1] - sigma[e, 1], lambda block, n: block + jnp.where(eye, ETA, 0.0)
         )
+        store(outgoing.at[e], (real, imag))
+
+    def one(flag):
+        return jnp.where(flag, 1, 0)
+
+    expected = depth + jnp.where(is_host, 0, ROW - 1) + one(starts_detour) + one(passes)
+    for e in range(e_local):
+        expected = expected + one(is_remote(e))
+    outputs = 2 * (ROW - 1) + jnp.where(is_near, 3, 4)
+    expected = expected + jnp.where(is_main, outputs, one(is_far))
+    pl.semaphore_wait(barrier, expected)
+
+    @pl.when(starts_detour)
+    def _():
+        for part in range(2):
+            detour_copy(part).start()
+
+    for e in range(e_local):
 
         @pl.when(is_remote(e))
         def _():
-            store(outgoing.at[e], (real, imag))
             base_copy(e).start()
 
+    for e in range(e_local):
+
+        @pl.when(jnp.logical_and(sends_coup(e), jnp.logical_not(passes)))
+        def _():
+            coup_copy(e).start()
+
+    for e in range(e_local):
+
         @pl.when(jnp.logical_not(is_remote(e)))
         def _():
-            store(base.at[place], (real, imag))
-
-    for e in range(e_local):
-
-        @pl.when(sends_coup(e))
-        def _():
+            base[place] = outgoing[e]
+            own_coup.start()
+
+    @pl.when(passes)
+    def _():
+        for part in range(2):
+            arrived(box_a.at[0, part], r_detour.at[part])
+            pass_in(part).start()
+        for e in range(e_local):
             coup_copy(e).start()
 
     def fill(e, carry):
@@ -302,7 +359,7 @@
         )
 
     def relayed(j):
-        return jnp.logical_and(is_far, (offset + j) // ROW != 2)
+        return (offset + j) // ROW != y
 
     def pass_copy(r, part):
         where = pl.ds(part * span, span)
@@ -400,7 +457,7 @@
                 for part in range(2):
                     now = jnp.logical_and(is_far, jnp.logical_not(relayed(j)))
                     if n == 0:
-                        now = jnp.logical_or(is_near, now)
+                        now = jnp.logical_or(jnp.logical_and(is_near, jnp.logical_not(relayed(j))), now)
 
                     @pl.when(jnp.logical_and(first_remote(j, part), now))
                     def _():
@@ -427,7 +484,7 @@
                 def one(j, carry):
                     for part in range(2):
 
-                        @pl.when(first_remote(j, part))
+                        @pl.when(jnp.logical_and(first_remote(j, part), jnp.logical_not(relayed(j))))
                         def _():
                             act(first_copy(j, part, n))
 
@@ -620,6 +677,16 @@
                 if a < adopt - 1:
                     adopt_green(a).wait_send()
 
+    @pl.when(starts_detour)
+    def _():
+        for part in range(2):
+            detour_copy(part).wait_send()
+
+    @pl.when(passes)
+    def _():
+        for part in range(2):
+            pass_in(part).wait_send()
+
     @pl.when(jnp.logical_not(is_host))
     def _():
         for r in range(ROW):
@@ -644,6 +711,20 @@
         second_copy(lax.rem(plane + turn, depth)).wait_send()
     last_copy.wait_send()
     arrived(out.at[:, other], r_last.at[0])
+
+
+def finish(source, target, done):
+    step = source.shape[0] // FINAL
+    copies = [
+        pltpu.make_async_copy(
+            source.at[n * step : (n + 1) * step], target.at[n * step : (n + 1) * step], done.at[n]
+        )
+        for n in range(FINAL)
+    ]
+    for copy in copies:
+        copy.start()
+    for copy in copies:
+        copy.wait()
 
 
 def body(onsite, hop, couple, sigma_in, shifts, mode_weight):
@@ -690,13 +771,20 @@
             sems(slots), sems(slots), sems(slots), sems(slots),
             sems(1), sems(1), sems(slots), sems(slots), sems(1), sems(1),
             sems(slots, 2, PIECES), sems(ROW, PIECES), sems(depth), sems(depth), sems(1), sems(1),
-            sems(2 * (CUT - BACK)), sems(CUT - BACK), sems(ROW, 2), pltpu.SemaphoreType.REGULAR,
+            sems(2 * (CUT - BACK)), sems(CUT - BACK), sems(ROW, 2), sems(2), sems(2), pltpu.SemaphoreType.REGULAR,
         ],
         compiler_params=pltpu.CompilerParams(
             collective_id=0, has_side_effects=True, vmem_limit_bytes=56 << 20
         ),
     )(shifts, mode_weight, onsite[0], hop[0, 0], couple[0, 0], sigma_in[:, 0])
-    return result[:, None]
+    final = pl.pallas_call(
+        finish,
+        out_shape=jax.ShapeDtypeStruct(result.shape, jnp.float32),
+        in_specs=[stay],
+        out_specs=stay,
+        scratch_shapes=[sems(FINAL)],
+    )(result)
+    return final[:, None]
 
 
 def solution(mesh):

time: 139 us -> 171 us (1.23)
  the two profiles are of different devices: /device:TPU:9 before, /device:TPU:1 now
where the time goes in v7:
time: 171 us
  Pallas kernels  171 us (100%)
    pallas_call x1, Pallas kernels, body(): pl.pallas_call(functools.partial(kernel, CUT, BACK, slabs, depth, e_local...  138 us
    pallas_call x1, Pallas kernels, body(): pl.pallas_call(finish, out_shape=jax.ShapeDtypeStruct(result.shape, jnp.f...  32.9 us

profile of v7, /device:TPU:1, one launch (start us, length us, event | category | flops | bytes accessed | tf_op | source)
XLA Modules:
  0.0 171.1 jit_solution(13978437626214006665)
XLA Ops:
  0.0 138.1 %shard_map.64.source = f32[16,2,32,256]{3,2,1,0:T(8,128)} custom-call(s32[4]{0:T(128)} %shifts.1, f32[2,4]{1,0:T(2,128)} %weights.1, f32[1,256]{1,0:T(1,128)} %bitcast.10, f32[2,256,256]{2,1,0:T(8,128)} %bitcast.8, f32[2,256,256]{2,1,0:T(8,128)} %bitcast.9, f32[2,2,256,256]{3,2,1,0:T(8,128)} %bitcast.7), custom_call_target="tpu_custom_call" | custom-call | tf_op jit(solution)/shard_map/pallas_call | solution.py:749
  138.1 32.9 %shard_map.65 = f32[16,2,32,256]{3,2,1,0:T(8,128)} custom-call(f32[16,2,32,256]{3,2,1,0:T(8,128)} %shard_map.64.source), custom_call_target="tpu_custom_call" | custom-call | tf_op jit(solution)/shard_map/pallas_call | solution.py:780

commit v8 on v7

--- a/solution.py
+++ b/solution.py
@@ -12,7 +12,8 @@
 CUT = 6
 BACK = 5
 PIECES = 4
-FINAL = 8
+ORDER = (2, 1, 3, 0)
+HASTE = 0
 MESH = pl.DeviceIdType.MESH
 
 
@@ -138,10 +139,14 @@
     def arrived(dst, recv_sem):
         send(dst, dst, s_hop.at[0], recv_sem, mom=other).wait_recv()
 
-    hop_load = pltpu.make_async_copy(hop_in, hop, s_in.at[0])
-    sigma_load = pltpu.make_async_copy(sigma_in, sigma, s_in.at[1])
-    hop_load.start()
-    sigma_load.start()
+    loads = []
+    for part in range(2):
+        loads.append(pltpu.make_async_copy(hop_in.at[part], hop.at[part], s_in.at[part]))
+        for e in range(e_local):
+            sem = s_in.at[2 + e * 2 + part]
+            loads.append(pltpu.make_async_copy(sigma_in.at[e, part], sigma.at[e, part], sem))
+    for item in loads:
+        item.start()
     barrier = pltpu.get_barrier_semaphore()
 
     def greet(**where):
@@ -201,8 +206,8 @@
     def _():
         greet(slab=near + x, mom=x // e_local)
 
-    hop_load.wait()
-    sigma_load.wait()
+    for item in loads:
+        item.wait()
     eye = eye_mask(half)
     place = slab - in_far * turn_at
 
@@ -266,7 +271,7 @@
 
     for e in range(e_local):
 
-        @pl.when(is_remote(e))
+        @pl.when(jnp.logical_and(is_remote(e), jnp.logical_not(passes)))
         def _():
             base_copy(e).start()
 
@@ -288,6 +293,10 @@
         for part in range(2):
             arrived(box_a.at[0, part], r_detour.at[part])
             pass_in(part).start()
+        for part in range(2):
+            pass_in(part).wait_send()
+        for e in range(e_local):
+            base_copy(e).start()
         for e in range(e_local):
             coup_copy(e).start()
 
@@ -332,7 +341,7 @@
         )
 
     def held(j, part):
-        late = offset + j >= slabs - ROW
+        late = jnp.logical_and(offset + j >= slabs - ROW, offset + j < slabs - HASTE)
         return jnp.logical_and(late, part == 1)
 
     def chain_copy(j):
@@ -342,7 +351,7 @@
         return send(h_chain.at[0], h_chain.at[turn_at], s_back.at[0], r_back.at[0], slab=slab - far)
 
     def piece(n):
-        return pl.ds(pl.multiple_of(lax.rem(plane * PIECES // depth + 1 + n, PIECES) * span, 8), span)
+        return pl.ds(pl.multiple_of(lax.rem(plane * PIECES // depth + ORDER[n], PIECES) * span, 8), span)
 
     def first_copy(j, part, n):
         return send(
@@ -350,23 +359,21 @@
             r_first.at[x, n], slab=offset + j, mom=part,
         )
 
-    def relay_copy(j, part, side):
-        where = pl.ds(side * half, half)
+    def relay_copy(j, part, n):
+        where = piece(n)
         return send(
             full.at[j, part, where], full.at[lax.rem(offset + j, ROW), part, where],
-            s_first.at[j, part, side], r_relay.at[lax.rem(offset + j, ROW), side],
+            s_first.at[j, part, n], r_relay.at[lax.rem(offset + j, ROW), n],
             slab=(offset + j) // ROW * ROW + x, mom=part,
         )
 
     def relayed(j):
         return (offset + j) // ROW != y
 
-    def pass_copy(r, part):
-        where = pl.ds(part * span, span)
-        order = lax.rem(part + 2 * PIECES - 1 - plane * PIECES // depth, PIECES)
+    def pass_copy(r, n):
         return send(
-            full.at[r, mom, where], gathered.at[x, where], s_first.at[r, 0, part],
-            r_first.at[x, order], slab=y * ROW + r,
+            full.at[r, mom, piece(n)], gathered.at[x, piece(n)], s_first.at[r, 0, n],
+            r_first.at[x, n], slab=y * ROW + r,
         )
 
     def is_first(j):
@@ -467,8 +474,8 @@
 
                 @pl.when(jnp.logical_and(relayed(j), jnp.logical_not(held(j, part))))
                 def _():
-                    for side in range(2):
-                        relay_copy(j, part, side).start()
+                    for n in range(PIECES):
+                        relay_copy(j, part, n).start()
 
                 @pl.when(jnp.logical_not(first_remote(j, part)))
                 def _():
@@ -506,8 +513,8 @@
 
                     @pl.when(held(j, part))
                     def _():
-                        for side in range(2):
-                            relay_copy(j, part, side).start()
+                        for n in range(PIECES):
+                            relay_copy(j, part, n).start()
 
                 return carry
 
@@ -578,18 +585,16 @@
     def _():
         def hand_on(turn, carry):
             r = ROW - 1 - turn
-            for side in range(2):
-                where = pl.ds(side * half, half)
-                arrived(full.at[r, mom, where], r_relay.at[r, side])
+            for n in range(PIECES):
+                arrived(full.at[r, mom, piece(n)], r_relay.at[r, n])
 
                 @pl.when(r != x)
                 def _():
-                    for part in range(side * PIECES // 2, (side + 1) * PIECES // 2):
-                        pass_copy(r, part).start()
+                    pass_copy(r, n).start()
 
                 @pl.when(r == x)
                 def _():
-                    gathered[x, where] = full[r, mom, where]
+                    gathered[x, piece(n)] = full[r, mom, piece(n)]
 
             return carry
 
@@ -607,7 +612,7 @@
         for e in range(e_local):
             summed[e, piece(n)] = gathered[e, piece(n)] + gathered[e_local + e, piece(n)]
         for k in range(per):
-            target = lax.rem(plane * PIECES // depth + 1 + n, PIECES) * per + k
+            target = lax.rem(plane * PIECES // depth + ORDER[n], PIECES) * per + k
 
             @pl.when(target != plane)
             def _():
@@ -630,9 +635,10 @@
         arrived(mixed.at[source], r_second.at[source])
         mixing(source, False)
 
-    out[:, mom] = total[...]
     last_copy = send(total, out.at[:, mom], s_last.at[0], r_last.at[0], mom=other)
     last_copy.start()
+    own_last = pltpu.make_async_copy(total, out.at[:, mom], s_last.at[1])
+    own_last.start()
 
     for e in range(e_local):
 
@@ -663,8 +669,8 @@
 
                 @pl.when(relayed(j))
                 def _():
-                    for side in range(2):
-                        relay_copy(j, part, side).wait_send()
+                    for n in range(PIECES):
+                        relay_copy(j, part, n).wait_send()
 
             return carry
 
@@ -682,19 +688,14 @@
         for part in range(2):
             detour_copy(part).wait_send()
 
-    @pl.when(passes)
-    def _():
-        for part in range(2):
-            pass_in(part).wait_send()
-
     @pl.when(jnp.logical_not(is_host))
     def _():
         for r in range(ROW):
 
             @pl.when(r != x)
             def _():
-                for part in range(PIECES):
-                    pass_copy(r, part).wait_send()
+                for n in range(PIECES):
+                    pass_copy(r, n).wait_send()
 
     @pl.when(is_helper)
     def _():
@@ -710,21 +711,8 @@
     for turn in range(1, depth):
         second_copy(lax.rem(plane + turn, depth)).wait_send()
     last_copy.wait_send()
+    own_last.wait()
     arrived(out.at[:, other], r_last.at[0])
-
-
-def finish(source, target, done):
-    step = source.shape[0] // FINAL
-    copies = [
-        pltpu.make_async_copy(
-            source.at[n * step : (n + 1) * step], target.at[n * step : (n + 1) * step], done.at[n]
-        )
-        for n in range(FINAL)
-    ]
-    for copy in copies:
-        copy.start()
-    for copy in copies:
-        copy.wait()
 
 
 def body(onsite, hop, couple, sigma_in, shifts, mode_weight):
@@ -750,7 +738,7 @@
         functools.partial(kernel, CUT, BACK, slabs, depth, e_local),
         out_shape=jax.ShapeDtypeStruct((total, 2, share, width), jnp.float32),
         in_specs=[smem, smem, vmem, stay, stay, stay],
-        out_specs=vmem,
+        out_specs=stay,
         scratch_shapes=[
             buffer(*block),
             buffer(e_local, *block),
@@ -766,25 +754,18 @@
             buffer(depth, e_local, share, width),
             buffer(total, share, width),
             pltpu.SMEM((total, total), jnp.float32),
-            sems(2),
+            sems(2 + 2 * e_local),
             sems(e_local), sems(slots), sems(e_local), sems(slots),
             sems(slots), sems(slots), sems(slots), sems(slots),
             sems(1), sems(1), sems(slots), sems(slots), sems(1), sems(1),
-            sems(slots, 2, PIECES), sems(ROW, PIECES), sems(depth), sems(depth), sems(1), sems(1),
-            sems(2 * (CUT - BACK)), sems(CUT - BACK), sems(ROW, 2), sems(2), sems(2), pltpu.SemaphoreType.REGULAR,
+            sems(slots, 2, PIECES), sems(ROW, PIECES), sems(depth), sems(depth), sems(2), sems(1),
+            sems(2 * (CUT - BACK)), sems(CUT - BACK), sems(ROW, PIECES), sems(2), sems(2), pltpu.SemaphoreType.REGULAR,
         ],
         compiler_params=pltpu.CompilerParams(
             collective_id=0, has_side_effects=True, vmem_limit_bytes=56 << 20
         ),
     )(shifts, mode_weight, onsite[0], hop[0, 0], couple[0, 0], sigma_in[:, 0])
-    final = pl.pallas_call(
-        finish,
-        out_shape=jax.ShapeDtypeStruct(result.shape, jnp.float32),
-        in_specs=[stay],
-        out_specs=stay,
-        scratch_shapes=[sems(FINAL)],
-    )(result)
-    return final[:, None]
+    return result[:, None]
 
 
 def solution(mesh):

time: 171 us -> 128 us (0.75)
  Pallas kernels: 171 us -> 126 us
  local copies, waits for them, and re-layouts: 0 us -> 2.31 us
    pallas_call x1 -> x0, Pallas kernels: 32.9 us -> none  [body(): pl.pallas_call(finish, out_shape=jax.ShapeDtypeStruct(result.shape, jnp.f...]
    pallas_call x1, Pallas kernels: 138 us -> 126 us  [body(): pl.pallas_call(functools.partial(kernel, CUT, BACK, slabs, depth, e_local...]
    unnamed x0 -> x1, local copies, waits for them, and re-layouts: none -> 2.31 us
where the time goes in v8:
time: 128 us
  Pallas kernels  126 us (98%)
  local copies, waits for them, and re-layouts  2.31 us (2%)
    pallas_call x1, Pallas kernels, body(): pl.pallas_call(functools.partial(kernel, CUT, BACK, slabs, depth, e_local...  126 us

profile of v8, /device:TPU:1, one launch (start us, length us, event | category | flops | bytes accessed | tf_op | source)
XLA Modules:
  0.0 128.2 jit_solution(7059344952815568482)
XLA Ops:
  0.0 125.8 %shard_map.64 = f32[16,2,32,256]{3,2,1,0:T(8,128)} custom-call(s32[4]{0:T(128)} %shifts.1, f32[2,4]{1,0:T(2,128)} %weights.1, f32[1,256]{1,0:T(1,128)} %bitcast.11, f32[2,256,256]{2,1,0:T(8,128)} %bitcast.9, f32[2,256,256]{2,1,0:T(8,128)} %bitcast.10, f32[2,2,256,256]{3,2,1,0:T(8,128)} %bitcast.8), custom_call_target="tpu_custom_call" | custom-call | tf_op jit(solution)/shard_map/pallas_call | solution.py:737
  125.8 2.3 %copy.9 = f32[16,1,2,32,256]{4,3,2,1,0:T(8,128)} copy(f32[16,1,2,32,256]{4,3,2,1,0:T(8,128)} %bitcast.7) | data formatting | bytes 2097152

commit v9 on v8

--- a/solution.py
+++ b/solution.py
@@ -13,7 +13,7 @@
 BACK = 5
 PIECES = 4
 ORDER = (2, 1, 3, 0)
-HASTE = 0
+HASTE = 3
 MESH = pl.DeviceIdType.MESH
 
 
@@ -88,6 +88,16 @@
     return ref[0], ref[1]
 
 
+def keep(ref, ready):
+    for n, parts in enumerate(ready):
+        ref[2 * n] = parts[0]
+        ref[2 * n + 1] = parts[1]
+
+
+def fetch(ref):
+    return tuple((ref[2 * n], ref[2 * n + 1]) for n in range(3))
+
+
 def store(ref, pair):
     ref[0] = pair[0]
     ref[1] = pair[1]
@@ -96,16 +106,16 @@
 def kernel(
     cut, turn_at, slabs, depth, e_local,
     shifts, weights, onsite, hop_in, couple, sigma_in, out,
-    hop, sigma, outgoing, left, box_a, box_b, box_c, box_d, box_e, gathered, summed, mixed, total,
+    hop, sigma, outgoing, left, box_a, box_b, box_c, box_d, box_e, h_first, h_second, gathered, summed, mixed, total,
     mix, s_in,
     s_base, r_base, s_coup, r_coup, s_hcoup, r_hcoup, s_hgreen, r_hgreen,
     s_hop, r_hop, s_chain, r_chain, s_back, r_back, s_first, r_first,
     s_second, r_second, s_last, r_last, s_adopt, r_adopt, r_relay, s_detour, r_detour, token,
 ):
     base = h_coup = h_adj = box_a
-    coup = h_green = h_first = box_b
+    coup = h_green = box_b
     green = h_chain = box_c
-    chain = h_second = box_d
+    chain = box_d
     full = box_e
     slab = lax.axis_index("slab")
     plane = lax.axis_index("energy")
@@ -341,8 +351,8 @@
         )
 
     def held(j, part):
-        late = jnp.logical_and(offset + j >= slabs - ROW, offset + j < slabs - HASTE)
-        return jnp.logical_and(late, part == 1)
+        late = offset + j >= slabs - ROW
+        return jnp.logical_and(late, jnp.logical_or(part == 1, offset + j < slabs - HASTE))
 
     def chain_copy(j):
         return send(h_chain.at[j + 1], chain.at[j], s_chain.at[j], r_chain.at[j], mom=other)
@@ -454,9 +464,9 @@
 
             @pl.when(jnp.logical_not(is_last(j)))
             def _():
-                arrived(chain.at[j], r_chain.at[j])
                 pair = load(green.at[j + 1])
                 ready = prep(pair)
+                arrived(chain.at[j], r_chain.at[j])
                 extra = mul(prep(mul(ready, prep(load(chain.at[j])))), ready)
                 store(full.at[j], (pair[0] + extra[0], pair[1] + extra[1]))
 
@@ -508,7 +518,8 @@
         def _():
             pl.semaphore_wait(token, 1)
 
-            def release(j, carry):
+            def release(turn, carry):
+                j = count - 1 - turn
                 for part in range(2):
 
                     @pl.when(held(j, part))
@@ -536,8 +547,8 @@
                 store(h_adj.at[j], adjoint)
                 arrived(h_green.at[j], r_hgreen.at[j])
                 ready = prep(load(h_green.at[j]))
-                store(h_first.at[j], mul(ready_left, ready))
-                store(h_second.at[j], mul(ready, ready_right))
+                keep(h_first.at[j], prep(mul(ready_left, ready)))
+                keep(h_second.at[j], prep(mul(ready, ready_right)))
 
             return carry
 
@@ -560,10 +571,10 @@
 
             @pl.when(jnp.logical_not(is_first(j)))
             def _():
-                extra = mul(prep(load(h_first.at[j])), prep(load(h_chain.at[j + 1])))
+                extra = mul(fetch(h_first.at[j]), prep(load(h_chain.at[j + 1])))
                 adjoint = load(h_adj.at[j])
                 sums = (adjoint[0] + extra[0], adjoint[1] + extra[1])
-                store(h_chain.at[j], mul(prep(sums), prep(load(h_second.at[j]))))
+                store(h_chain.at[j], mul(prep(sums), fetch(h_second.at[j])))
 
             return carry
 
@@ -584,7 +595,7 @@
     @pl.when(jnp.logical_not(is_host))
     def _():
         def hand_on(turn, carry):
-            r = ROW - 1 - turn
+            r = jnp.where(jnp.logical_and(y == 1, turn >= 2), turn - 2, ROW - 1 - turn)
             for n in range(PIECES):
                 arrived(full.at[r, mom, piece(n)], r_relay.at[r, n])
 
@@ -724,6 +735,7 @@
     share = width // depth
     block = (2, width, width)
     slots = max(CUT, slabs - BACK)
+    spare = max(1, CUT - BACK)
 
     def buffer(*shape):
         return pltpu.VMEM(shape, jnp.float32)
@@ -749,6 +761,8 @@
             buffer(slots + 1, *block),
             buffer(slots, *block),
             buffer(slots, *block),
+            pltpu.VMEM((slots, 6, width, width), jnp.bfloat16),
+            pltpu.VMEM((slots, 6, width, width), jnp.bfloat16),
             buffer(ROW, width, width),
             buffer(e_local, width, width),
             buffer(depth, e_local, share, width),
@@ -759,7 +773,7 @@
             sems(slots), sems(slots), sems(slots), sems(slots),
             sems(1), sems(1), sems(slots), sems(slots), sems(1), sems(1),
             sems(slots, 2, PIECES), sems(ROW, PIECES), sems(depth), sems(depth), sems(2), sems(1),
-            sems(2 * (CUT - BACK)), sems(CUT - BACK), sems(ROW, PIECES), sems(2), sems(2), pltpu.SemaphoreType.REGULAR,
+            sems(2 * spare), sems(spare), sems(ROW, PIECES), sems(2), sems(2), pltpu.SemaphoreType.REGULAR,
         ],
         compiler_params=pltpu.CompilerParams(
             collective_id=0, has_side_effects=True, vmem_limit_bytes=56 << 20

time: 128 us -> 127 us (level)
  no operation moved by 1% of the time
where the time goes in v9:
time: 127 us
  Pallas kernels  125 us (98%)
  local copies, waits for them, and re-layouts  2.31 us (2%)
    pallas_call x1, Pallas kernels, body(): pl.pallas_call(functools.partial(kernel, CUT, BACK, slabs, depth, e_local...  125 us

profile of v9, /device:TPU:1, one launch (start us, length us, event | category | flops | bytes accessed | tf_op | source)
XLA Modules:
  0.0 126.9 jit_solution(3770239430767451862)
XLA Ops:
  0.0 124.6 %shard_map.64 = f32[16,2,32,256]{3,2,1,0:T(8,128)} custom-call(s32[4]{0:T(128)} %shifts.1, f32[2,4]{1,0:T(2,128)} %weights.1, f32[1,256]{1,0:T(1,128)} %bitcast.11, f32[2,256,256]{2,1,0:T(8,128)} %bitcast.9, f32[2,256,256]{2,1,0:T(8,128)} %bitcast.10, f32[2,2,256,256]{3,2,1,0:T(8,128)} %bitcast.8), custom_call_target="tpu_custom_call" | custom-call | tf_op jit(solution)/shard_map/pallas_call | solution.py:749
  124.6 2.3 %copy.9 = f32[16,1,2,32,256]{4,3,2,1,0:T(8,128)} copy(f32[16,1,2,32,256]{4,3,2,1,0:T(8,128)} %bitcast.7) | data formatting | bytes 2097152

commit v10 on v9

--- a/solution.py
+++ b/solution.py
@@ -519,17 +519,18 @@
             pl.semaphore_wait(token, 1)
 
             def release(turn, carry):
-                j = count - 1 - turn
+                j = lax.rem(2 * count - 1 - turn, count)
                 for part in range(2):
-
-                    @pl.when(held(j, part))
+                    mine = jnp.logical_and(held(j, part), turn // count == part)
+
+                    @pl.when(mine)
                     def _():
                         for n in range(PIECES):
                             relay_copy(j, part, n).start()
 
                 return carry
 
-            lax.fori_loop(0, count, release, 0)
+            lax.fori_loop(0, 2 * count, release, 0)
 
     @pl.when(is_helper)
     def _():

time: 127 us -> 127 us (level)
  no operation moved by 1% of the time
where the time goes in v10:
time: 127 us
  Pallas kernels  125 us (98%)
  local copies, waits for them, and re-layouts  2.31 us (2%)
    pallas_call x1, Pallas kernels, body(): pl.pallas_call(functools.partial(kernel, CUT, BACK, slabs, depth, e_local...  125 us

profile of v10, /device:TPU:1, one launch (start us, length us, event | category | flops | bytes accessed | tf_op | source)
XLA Modules:
  0.0 126.9 jit_solution(13754174153177527169)
XLA Ops:
  0.0 124.6 %shard_map.64 = f32[16,2,32,256]{3,2,1,0:T(8,128)} custom-call(s32[4]{0:T(128)} %shifts.1, f32[2,4]{1,0:T(2,128)} %weights.1, f32[1,256]{1,0:T(1,128)} %bitcast.11, f32[2,256,256]{2,1,0:T(8,128)} %bitcast.9, f32[2,256,256]{2,1,0:T(8,128)} %bitcast.10, f32[2,2,256,256]{3,2,1,0:T(8,128)} %bitcast.8), custom_call_target="tpu_custom_call" | custom-call | tf_op jit(solution)/shard_map/pallas_call | solution.py:750
  124.6 2.3 %copy.9 = f32[16,1,2,32,256]{4,3,2,1,0:T(8,128)} copy(f32[16,1,2,32,256]{4,3,2,1,0:T(8,128)} %bitcast.7) | data formatting | bytes 2097152

commit v11 on v10

--- a/solution.py
+++ b/solution.py
@@ -473,7 +473,7 @@
             for n in range(PIECES):
                 for part in range(2):
                     now = jnp.logical_and(is_far, jnp.logical_not(relayed(j)))
-                    if n == 0:
+                    if n < 2:
                         now = jnp.logical_or(jnp.logical_and(is_near, jnp.logical_not(relayed(j))), now)
 
                     @pl.when(jnp.logical_and(first_remote(j, part), now))
@@ -509,9 +509,10 @@
 
                 lax.fori_loop(0, count, one, 0)
 
-            for n in range(1, PIECES):
+            for n in range(2, PIECES):
                 sweep(n, lambda copy: copy.start())
-                sweep(n - 1, lambda copy: copy.wait_send())
+                sweep(n - 2, lambda copy: copy.wait_send())
+            sweep(PIECES - 2, lambda copy: copy.wait_send())
             sweep(PIECES - 1, lambda copy: copy.wait_send())
 
         @pl.when(is_far)

time: 127 us -> 127 us (level)
  no operation moved by 1% of the time
where the time goes in v11:
time: 127 us
  Pallas kernels  125 us (98%)
  local copies, waits for them, and re-layouts  2.31 us (2%)
    pallas_call x1, Pallas kernels, body(): pl.pallas_call(functools.partial(kernel, CUT, BACK, slabs, depth, e_local...  125 us

profile of v11, /device:TPU:1, one launch (start us, length us, event | category | flops | bytes accessed | tf_op | source)
XLA Modules:
  0.0 126.9 jit_solution(15500260596573354516)
XLA Ops:
  0.0 124.6 %shard_map.64 = f32[16,2,32,256]{3,2,1,0:T(8,128)} custom-call(s32[4]{0:T(128)} %shifts.1, f32[2,4]{1,0:T(2,128)} %weights.1, f32[1,256]{1,0:T(1,128)} %bitcast.11, f32[2,256,256]{2,1,0:T(8,128)} %bitcast.9, f32[2,256,256]{2,1,0:T(8,128)} %bitcast.10, f32[2,2,256,256]{3,2,1,0:T(8,128)} %bitcast.8), custom_call_target="tpu_custom_call" | custom-call | tf_op jit(solution)/shard_map/pallas_call | solution.py:751
  124.6 2.3 %copy.9 = f32[16,1,2,32,256]{4,3,2,1,0:T(8,128)} copy(f32[16,1,2,32,256]{4,3,2,1,0:T(8,128)} %bitcast.7) | data formatting | bytes 2097152
